TPU v7x, 32 devices: a whole 2x2x4 slice. The times are simulated.
32 devices in a mesh: dp: 4 (over y, x), seq: 2 (over core), tensor: 4 (over z).
Axes of the slice: x: 2, y: 2, z: 4, core: 2. Of those that a mesh axis runs over, the one named last changes fastest.
Arguments:
- block_input: bfloat16 [8, 256, 1024], P('dp', 'seq'), may hold values from -6 to 6
- cotangent: bfloat16 [8, 256, 1024], P('dp', 'seq'), may hold values from -6 to 6
- segments: int32 [8, 256], P('dp', 'seq'), may hold values from 0 to 3, as said below
- positions: int32 [8, 256], P('dp', 'seq'), may hold values from 0 to 255, as said below
- w_qkv: bfloat16 [3, 1024, 1024], P(None, ('dp', 'seq'), 'tensor')
- qkv_bias: float32 [3, 1024], P(None, 'tensor'), may hold values from -3 to 3
- w_out: bfloat16 [1024, 1024], P('tensor', ('dp', 'seq')), may hold values from -1.5 to 1.5
- w_fc1: bfloat16 [1024, 4096], P(('dp', 'seq'), 'tensor'), may hold values from -0.1875 to 0.1875
- fc1_bias: float32 [4096], P('tensor'), may hold values from -3 to 3
- w_fc2: bfloat16 [4096, 1024], P('tensor', ('dp', 'seq')), may hold values from -0.09375 to 0.09375
- ln_gains: float32 [2, 1024], replicated, may hold values from 0.5 to 1.5
- row_biases: float32 [4, 1024], replicated, may hold values from -3 to 3
Outputs:
- output: bfloat16 [8, 256, 1024], P('dp', 'seq')
- grad_input: float32 [8, 256, 1024], P('dp', 'seq')
- grad_w_qkv: float32 [3, 1024, 1024], P(None, ('dp', 'seq'), 'tensor')
- grad_w_out: float32 [1024, 1024], P('tensor', ('dp', 'seq'))
- grad_w_fc1: float32 [1024, 4096], P(('dp', 'seq'), 'tensor')
- grad_w_fc2: float32 [4096, 1024], P('tensor', ('dp', 'seq'))
- grad_qkv_bias: float32 [3, 1024], P(None, 'tensor')
- grad_fc1_bias: float32 [4096], P('tensor')
- grad_ln_gains: float32 [2, 1024], replicated
- grad_row_biases: float32 [4, 1024], replicated
Inputs may be any that keep to these rules, and one draw needn't show every extreme that they name: `segments`: segment numbers start at 0 and never fall along a sequence; a rise marks the start of a document; the first sequence is one document and the second reaches document number 3. `positions`: each token's position counts the tokens before it in its own document.
All inputs are finite; a program needn't handle non-finite values.
Results may differ from a plain program's by a relative error of at most 0.02.
Values may be sent and summed in bfloat16 or wider, within the bound.
A program may use at most 128 MiB of HBM per device.

v0:
```python
import math

import jax
import jax.numpy as jnp
from jax import lax
from jax.sharding import PartitionSpec as P

HD = 64
ROT = 16


norm_eps = 1e-05
neg_big = -1e30
inv_root_two = 0.7071067811865476
inv_root_tau = 0.3989422804014327


def layer_norm(values, gain, shift):
    centred = values - jnp.mean(values, axis=-1, keepdims=True)
    inv_std = lax.rsqrt(jnp.mean(centred * centred, axis=-1, keepdims=True) + norm_eps)
    normed = centred * inv_std
    return (normed * gain + shift, normed, inv_std)


def norm_back(grad_out, normed, inv_std, gain):
    scaled = grad_out * gain
    centre = jnp.mean(scaled, axis=-1, keepdims=True)
    slope = jnp.mean(scaled * normed, axis=-1, keepdims=True)
    return inv_std * (scaled - centre - normed * slope)


def gelu_pair(pre_act):
    cumul = 0.5 * (1.0 + lax.erf(pre_act * inv_root_two))
    return (pre_act * cumul, cumul + pre_act * inv_root_tau * jnp.exp(-0.5 * pre_act * pre_act))


def rotary_tables(positions):
    half_rot = ROT // 2
    freqs = 10000.0 ** (-2.0 * jnp.arange(half_rot).astype(jnp.float32) / ROT)
    angles = positions.astype(jnp.float32)[..., None] * freqs
    cosine = jnp.cos(angles)
    sine = jnp.sin(angles)
    return (
        jnp.concatenate([cosine, cosine], -1)[..., None, :],
        jnp.concatenate([sine, sine], -1)[..., None, :],
    )


def rotate(tensor, cosine, sine):
    half_rot = ROT // 2
    head = tensor[..., :ROT]
    turned = jnp.concatenate([-head[..., half_rot:], head[..., :half_rot]], -1)
    return jnp.concatenate([head * cosine + turned * sine, tensor[..., ROT:]], -1)


def unrotate(grads, cosine, sine):
    half_rot = ROT // 2
    head = grads[..., :ROT]
    times_sine = head * sine
    back = jnp.concatenate([times_sine[..., half_rot:], -times_sine[..., :half_rot]], -1)
    return jnp.concatenate([head * cosine + back, grads[..., ROT:]], -1)


def gather_keys(keys_flat, values_in, segments):
    return (
        lax.all_gather(keys_flat, "seq", axis=1, tiled=True),
        lax.all_gather(values_in, "seq", axis=1, tiled=True),
        lax.all_gather(segments, "seq", axis=1, tiled=True),
    )


def pair_terms(
    query_blk,
    query_pos,
    query_seg,
    key_blk,
    value_blk,
    key_pos,
    key_seg,
    grad_blk,
    log_blk,
    delta_blk,
    scale,
):
    scores = (
        jnp.einsum("sqhd,skhd->shqk", query_blk, key_blk, preferred_element_type=jnp.float32)
        * scale
    )
    same_doc = query_seg[:, None, :, None] == key_seg[:, None, None, :]
    earlier = key_pos[None, None, None, :] <= query_pos[None, None, :, None]
    probs = jnp.where(same_doc & earlier, jnp.exp(scores - log_blk[..., None]), 0.0)
    grad_p = jnp.einsum("sqhd,skhd->shqk", grad_blk, value_blk, preferred_element_type=jnp.float32)
    grad_s = (probs * (grad_p - delta_blk[..., None])).astype(jnp.bfloat16)
    return (probs, grad_s)


def shards(
    block_input,
    cotangent,
    segments,
    positions,
    w_qkv,
    qkv_bias,
    w_out,
    w_fc1,
    fc1_bias,
    w_fc2,
    ln_gains,
    row_biases,
):
    seqs_here, rows_here, width = block_input.shape
    heads_here = w_qkv.shape[2] // HD
    flat_width = heads_here * HD
    scale = HD ** (-0.5)
    shape_heads = (seqs_here, rows_here, heads_here, HD)
    forward_weights = (
        lax.all_gather(w_qkv, ("dp", "seq"), axis=1, tiled=True),
        lax.all_gather(w_out, ("dp", "seq"), axis=1, tiled=True),
        lax.all_gather(w_fc1, ("dp", "seq"), axis=0, tiled=True),
        lax.all_gather(w_fc2, ("dp", "seq"), axis=1, tiled=True),
    )
    query_key_value_gathered, output_weight_gathered, up_weight_gathered, down_weight_gathered = (
        forward_weights
    )
    inputs_f = block_input.astype(jnp.float32)
    first_out, first_normed, first_inv = layer_norm(inputs_f, ln_gains[0], row_biases[0])
    second_out, second_normed, second_inv = layer_norm(inputs_f, ln_gains[1], row_biases[1])
    first_norm_input = first_out.astype(jnp.bfloat16)
    second_norm_input = second_out.astype(jnp.bfloat16)
    projected = (
        jnp.einsum(
            "bxf,kfh->kbxh",
            first_norm_input,
            query_key_value_gathered,
            preferred_element_type=jnp.float32,
        )
        + qkv_bias[:, None, None, :]
    )
    cosine, sine = rotary_tables(positions)
    queries = rotate(projected[0].reshape(shape_heads), cosine, sine).astype(jnp.bfloat16)
    keys_flat = (
        rotate(projected[1].reshape(shape_heads), cosine, sine)
        .astype(jnp.bfloat16)
        .reshape(seqs_here, rows_here, flat_width)
    )
    values_in = projected[2].astype(jnp.bfloat16)
    query_pos = lax.axis_index("seq") * rows_here + jnp.arange(rows_here)

    def block_scores(key_block, seg_block, key_start):
        count = key_block.shape[1]
        keys_heads = key_block.reshape(seqs_here, count, heads_here, HD)
        scores = (
            jnp.einsum("sqhd,skhd->shqk", queries, keys_heads, preferred_element_type=jnp.float32)
            * scale
        )
        key_pos = key_start + jnp.arange(count)
        same_doc = segments[:, None, :, None] == seg_block[:, None, None, :]
        earlier = key_pos[None, None, None, :] <= query_pos[None, None, :, None]
        return (scores, same_doc & earlier)

    start_state = (
        jnp.full((seqs_here, heads_here, rows_here), neg_big, jnp.float32),
        jnp.zeros((seqs_here, heads_here, rows_here), jnp.float32),
        jnp.zeros((seqs_here, heads_here, rows_here, HD), jnp.float32),
    )
    key_part = lax.all_gather(keys_flat, "seq", axis=1, tiled=True)
    value_part = lax.all_gather(values_in, "seq", axis=1, tiled=True)
    seg_part = lax.all_gather(segments, "seq", axis=1, tiled=True)
    count = key_part.shape[1]
    attend_block = math.gcd(count, 512)

    def step_block(block_idx, state):
        run_max, run_sum, accum = state
        offset = block_idx * attend_block
        key_block = lax.dynamic_slice_in_dim(key_part, offset, attend_block, 1)
        value_block = lax.dynamic_slice_in_dim(value_part, offset, attend_block, 1).reshape(
            seqs_here, attend_block, heads_here, HD
        )
        seg_block = lax.dynamic_slice_in_dim(seg_part, offset, attend_block, 1)
        scores, allowed = block_scores(key_block, seg_block, offset)
        new_max = jnp.maximum(run_max, jnp.max(jnp.where(allowed, scores, neg_big), axis=-1))
        factor = jnp.exp(run_max - new_max)
        expo = jnp.where(allowed, jnp.exp(scores - new_max[..., None]), 0.0)
        new_sum = run_sum * factor + jnp.sum(expo, axis=-1)
        update = jnp.einsum(
            "shqk,skhd->shqd",
            expo.astype(jnp.bfloat16),
            value_block,
            preferred_element_type=jnp.float32,
        )
        return (new_max, new_sum, accum * factor[..., None] + update)

    run_max, run_sum, accum = lax.fori_loop(0, count // attend_block, step_block, start_state)
    log_sum = run_max + jnp.log(run_sum)
    attention_context = (
        (accum / run_sum[..., None])
        .transpose(0, 2, 1, 3)
        .reshape(seqs_here, rows_here, flat_width)
        .astype(jnp.bfloat16)
    )
    pre_act = (
        jnp.einsum(
            "vrk,kt->vrt", second_norm_input, up_weight_gathered, preferred_element_type=jnp.float32
        )
        + fc1_bias
    )
    activ, gelu_slope = gelu_pair(pre_act)
    hidden_activation = activ.astype(jnp.bfloat16)
    partial_output_sum = jnp.einsum(
        "qhw,wj->qhj", attention_context, output_weight_gathered, preferred_element_type=jnp.float32
    )
    partial_output_sum = partial_output_sum + jnp.einsum(
        "qzg,gc->qzc", hidden_activation, down_weight_gathered, preferred_element_type=jnp.float32
    )
    branches = lax.psum(partial_output_sum.astype(jnp.bfloat16), "tensor").astype(jnp.float32)
    output = (inputs_f + branches + row_biases[2] + row_biases[3]).astype(jnp.bfloat16)
    query_key_value_backward, output_weight_backward, up_weight_backward, down_weight_backward = (
        lax.all_gather(w_qkv, ("dp", "seq"), axis=1, tiled=True),
        lax.all_gather(w_out, ("dp", "seq"), axis=1, tiled=True),
        lax.all_gather(w_fc1, ("dp", "seq"), axis=0, tiled=True),
        lax.all_gather(w_fc2, ("dp", "seq"), axis=1, tiled=True),
    )
    grad_f = cotangent.astype(jnp.float32)
    gradient_output_weight = jnp.einsum(
        "bxz,bxe->ze", attention_context, cotangent, preferred_element_type=jnp.float32
    )
    grad_context = jnp.einsum(
        "zpi,xi->zpx", cotangent, output_weight_backward, preferred_element_type=jnp.float32
    ).astype(jnp.bfloat16)
    gradient_down_weight = jnp.einsum(
        "tzi,tzo->io", hidden_activation, cotangent, preferred_element_type=jnp.float32
    )
    grad_pre = (
        jnp.einsum(
            "hvg,rg->hvr", cotangent, down_weight_backward, preferred_element_type=jnp.float32
        )
        * gelu_slope
    )
    gradient_hidden_input = grad_pre.astype(jnp.bfloat16)
    grad_fc1_w = jnp.einsum(
        "mxa,mxr->ar", second_norm_input, gradient_hidden_input, preferred_element_type=jnp.float32
    )
    grad_second = jnp.einsum(
        "ikq,uq->iku", gradient_hidden_input, up_weight_backward, preferred_element_type=jnp.float32
    )
    grad_ctx_heads = grad_context.reshape(shape_heads)
    delta = jnp.sum(
        grad_ctx_heads.astype(jnp.float32)
        * attention_context.reshape(shape_heads).astype(jnp.float32),
        axis=-1,
    ).transpose(0, 2, 1)
    key_all, value_all, seg_all = gather_keys(keys_flat, values_in, segments)
    total_len = key_all.shape[1]
    block = math.gcd(total_len, 512)

    def key_slices(offset):
        key_block = lax.dynamic_slice_in_dim(key_all, offset, block, 1).reshape(
            seqs_here, block, heads_here, HD
        )
        value_block = lax.dynamic_slice_in_dim(value_all, offset, block, 1).reshape(
            seqs_here, block, heads_here, HD
        )
        seg_block = lax.dynamic_slice_in_dim(seg_all, offset, block, 1)
        return (key_block, value_block, seg_block)

    def back_block(block_idx, state):
        grad_q, grad_key_all, grad_value_all = state
        offset = block_idx * block
        key_block, value_block, seg_block = key_slices(offset)
        probs, grad_s = pair_terms(
            queries,
            query_pos,
            segments,
            key_block,
            value_block,
            offset + jnp.arange(block),
            seg_block,
            grad_ctx_heads,
            log_sum,
            delta,
            scale,
        )
        grad_v = jnp.einsum(
            "shqk,sqhd->skhd",
            probs.astype(jnp.bfloat16),
            grad_ctx_heads,
            preferred_element_type=jnp.float32,
        )
        grad_q = (
            grad_q
            + jnp.einsum("shqk,skhd->sqhd", grad_s, key_block, preferred_element_type=jnp.float32)
            * scale
        )
        grad_k = (
            jnp.einsum("shqk,sqhd->skhd", grad_s, queries, preferred_element_type=jnp.float32)
            * scale
        )
        grad_key_all = lax.dynamic_update_slice_in_dim(
            grad_key_all, grad_k.reshape(seqs_here, block, flat_width), offset, 1
        )
        grad_value_all = lax.dynamic_update_slice_in_dim(
            grad_value_all, grad_v.reshape(seqs_here, block, flat_width), offset, 1
        )
        return (grad_q, grad_key_all, grad_value_all)

    back_start = (
        jnp.zeros(shape_heads, jnp.float32),
        jnp.zeros((seqs_here, total_len, flat_width), jnp.float32),
        jnp.zeros((seqs_here, total_len, flat_width), jnp.float32),
    )
    grad_q, grad_key_all, grad_value_all = lax.fori_loop(
        0, total_len // block, back_block, back_start
    )
    grad_key_here, grad_value_here = (
        lax.psum_scatter(
            grad_key_all.astype(jnp.bfloat16), "seq", scatter_dimension=1, tiled=True
        ).astype(jnp.float32),
        lax.psum_scatter(
            grad_value_all.astype(jnp.bfloat16), "seq", scatter_dimension=1, tiled=True
        ).astype(jnp.float32),
    )
    grad_proj = jnp.stack(
        [
            unrotate(grad_q, cosine, sine).reshape(seqs_here, rows_here, flat_width),
            unrotate(grad_key_here.reshape(shape_heads), cosine, sine).reshape(
                seqs_here, rows_here, flat_width
            ),
            grad_value_here,
        ]
    )
    grad_bias_qkv = jnp.sum(grad_proj, axis=(1, 2))
    gradient_projection_input = grad_proj.astype(jnp.bfloat16)
    grad_qkv_w = jnp.einsum(
        "ink,oint->okt",
        first_norm_input,
        gradient_projection_input,
        preferred_element_type=jnp.float32,
    )
    grad_first = jnp.einsum(
        "etbp,eop->tbo",
        gradient_projection_input,
        query_key_value_backward,
        preferred_element_type=jnp.float32,
    )
    grad_first, grad_second = (
        lax.psum(grad_first.astype(jnp.bfloat16), "tensor").astype(jnp.float32),
        lax.psum(grad_second.astype(jnp.bfloat16), "tensor").astype(jnp.float32),
    )
    grad_input = (
        grad_f
        + norm_back(grad_first, first_normed, first_inv, ln_gains[0])
        + norm_back(grad_second, second_normed, second_inv, ln_gains[1])
    )
    gain_terms = jnp.stack(
        [
            jnp.sum(grad_first * first_normed, axis=(0, 1)),
            jnp.sum(grad_second * second_normed, axis=(0, 1)),
        ]
    )
    row_terms = jnp.stack(
        [
            jnp.sum(grad_first, axis=(0, 1)),
            jnp.sum(grad_second, axis=(0, 1)),
            jnp.sum(grad_f, axis=(0, 1)),
            jnp.sum(grad_f, axis=(0, 1)),
        ]
    )
    bias_sums = lax.psum(
        (grad_bias_qkv, jnp.sum(grad_pre, axis=(0, 1)), gain_terms, row_terms), ("dp", "seq")
    )
    weight_sums = (
        lax.psum_scatter(grad_qkv_w, ("dp", "seq"), scatter_dimension=1, tiled=True),
        lax.psum_scatter(gradient_output_weight, ("dp", "seq"), scatter_dimension=1, tiled=True),
        lax.psum_scatter(grad_fc1_w, ("dp", "seq"), scatter_dimension=0, tiled=True),
        lax.psum_scatter(gradient_down_weight, ("dp", "seq"), scatter_dimension=1, tiled=True),
    )
    return (
        output,
        grad_input,
        weight_sums[0],
        weight_sums[1],
        weight_sums[2],
        weight_sums[3],
        bias_sums[0],
        bias_sums[1],
        bias_sums[2],
        bias_sums[3],
    )


def solution(mesh):
    return jax.shard_map(
        shards,
        mesh=mesh,
        in_specs=(
            P("dp", "seq", None),
            P("dp", "seq", None),
            P("dp", "seq"),
            P("dp", "seq"),
            P(None, ("dp", "seq"), "tensor"),
            P(None, "tensor"),
            P("tensor", ("dp", "seq")),
            P(("dp", "seq"), "tensor"),
            P("tensor"),
            P("tensor", ("dp", "seq")),
            P(),
            P(),
        ),
        out_specs=(
            P("dp", "seq", None),
            P("dp", "seq", None),
            P(None, ("dp", "seq"), "tensor"),
            P("tensor", ("dp", "seq")),
            P(("dp", "seq"), "tensor"),
            P("tensor", ("dp", "seq")),
            P(None, "tensor"),
            P("tensor"),
            P(),
            P(),
        ),
        check_vma=False,
    )
```

profile of v0, /device:TPU:0, one launch (start us, length us, event | category | flops | bytes accessed | tf_op | source)
XLA Modules:
  0.0 412.7 jit_solution(13433053082500771721)
XLA Ops:
  8.7 11.7 %all_gather.32 = bf16[256,1024]{1,0:T(8,128)(2,1)S(1)} all-gather(bf16[256,128]{1,0:T(8,128)(2,1)} %param.18), channel_id=1, replica_groups=mesh['dp'=4,'seq'=2,'tensor'=4] {'dp','seq'}, dimensions={1}, use_global_device_ids=true | all-gather | bytes 589824 | tf_op jit(solution)/shard_map/all_gather | solution.py:118
  20.4 1.4 convolution_convert_fusion.1
  22.0 1.8 all_gather.28
  25.3 13.0 %all-gather.5.cloned.1.call-done = bf16[3,1024,256]{2,1,0:T(8,128)(2,1)} async-done(((bf16[3,128,256]{2,1,0:T(8,128)(2,1)}), bf16[3,1024,256]{2,1,0:T(8,128)(2,1)}) %all-gather.5.cloned.1.call-update) | async-done | bytes 1572880 | tf_op jit(solution)/shard_map/all_gather | solution.py:117
  38.3 2.1 fusion.39
  41.6 2.0 all_gather.30
  45.5 2.0 all-gather
  48.7 1.5 fusion.31
  51.4 1.3 convolution_convert_fusion
  55.1 4.1 %reduce-scatter.19.cloned.1.call-done = bf16[128,512]{1,0:T(8,128)(2,1)} async-done(((bf16[256,512]{1,0:T(8,128)(2,1)}), bf16[128,512]{1,0:T(8,128)(2,1)}) %reduce-scatter.19.cloned.1.call-update) | async-done | bytes 131088
  60.8 10.1 %reduce-scatter.9.cloned.1.call-done = bf16[2,128,256]{2,1,0:T(8,128)(2,1)} async-done(((bf16[2,256,256]{2,1,0:T(8,128)(2,1)}), bf16[2,128,256]{2,1,0:T(8,128)(2,1)}) %reduce-scatter.9.cloned.1.call-update) | async-done | bytes 131088 | tf_op jit(solution)/shard_map/reduce_scatter | solution.py:318
  71.9 2.8 fusion.28
  74.7 26.9 %all-gather.7.cloned.1.call-done = bf16[1024,1024]{1,0:T(8,128)(2,1)} async-done(((bf16[128,1024]{1,0:T(8,128)(2,1)}), bf16[1024,1024]{1,0:T(8,128)(2,1)}) %all-gather.7.cloned.1.call-update) | async-done | bytes 2097168 | tf_op jit(solution)/shard_map/all_gather | solution.py:119
  101.6 2.3 fusion.22
  104.0 27.5 %all-gather.9.cloned.1.call-done = bf16[1024,1024]{1,0:T(8,128)(2,1)} async-done(((bf16[1024,128]{1,0:T(8,128)(2,1)}), bf16[1024,1024]{1,0:T(8,128)(2,1)}) %all-gather.9.cloned.1.call-update) | async-done | bytes 2097168 | tf_op jit(solution)/shard_map/all_gather | solution.py:120
  131.5 2.4 fusion.2
  134.0 1.1 fusion.35
  135.1 1.6 fusion.111
  136.7 1.5 fusion.32
  138.3 3.3 convolution_bitcast_fusion.2
  141.7 1.3 convolution_bitcast_fusion.3
  143.0 3.5 convolution_bitcast_fusion.1
  146.7 2.7 convolution_bitcast_fusion
  149.6 57.9 %all-reduce.4.cloned.1.call-done = (bf16[2,128,1024]{2,1,0:T(8,128)(2,1)}, bf16[2,128,1024]{2,1,0:T(8,128)(2,1)}, bf16[2,128,1024]{2,1,0:T(8,128)(2,1)}) async-done(((bf16[2,128,1024]{2,1,0:T(8,128)(2,1)}, bf16[2,128,1024]{2,1,0:T(8,128)(2,1)}, bf16[2,128,1024]{2,1,0:T(8,128)(2,1)}), (bf16[2,128,1024]{2,1,0:T(8,128)(2,1)}, bf16[2,128,1024]{2,1,0:T(8,128)(2,1)}, ...) | async-done | bytes 1572880 | tf_op jit(solution)/shard_map/psum | solution.py:215
  207.5 2.2 fusion.68
  209.7 3.4 convert_reduce_fusion.3
  213.2 24.2 %all-reduce = (f32[3,256]{1,0:T(4,128)}, f32[1024]{0:T(1024)}, f32[2,1024]{1,0:T(2,128)}, f32[4,1024]{1,0:T(4,128)}) all-reduce(f32[3,256]{1,0:T(4,128)S(1)} %fusion.76, f32[1024]{0:T(1024)S(1)} %copy-done.16, f32[2,1024]{1,0:T(2,128)S(1)} %pad_maximum_fusion.10, ...), channel_id=1, replica_groups=mesh['dp'=4,'seq'=2,'tensor'=4] {'dp','seq'}, use_global_device_ids=true, to_apply=%region_19.20 | all-reduce | flops 7936 | bytes 63488 | tf_op jit(solution)/shard_map/psum | solution.py:368
  237.4 18.7 %reduce-scatter.11.cloned.1.call-done = f32[3,128,256]{1,2,0:T(8,128)} async-done(((f32[3,1024,256]{1,2,0:T(8,128)}), f32[3,128,256]{1,2,0:T(8,128)}) %reduce-scatter.11.cloned.1.call-update) | async-done | bytes 393232 | tf_op jit(solution)/shard_map/reduce_scatter | solution.py:372
  256.1 1.9 copy.65
  258.0 37.8 %reduce-scatter.13.cloned.1.call-done = f32[256,128]{1,0:T(8,128)} async-done(((f32[256,1024]{1,0:T(8,128)}), f32[256,128]{1,0:T(8,128)}) %reduce-scatter.13.cloned.1.call-update) | async-done | bytes 131088 | tf_op jit(solution)/shard_map/reduce_scatter | solution.py:373
  295.8 55.1 %reduce-scatter.15.cloned.1.call-done = f32[128,1024]{1,0:T(8,128)} async-done(((f32[1024,1024]{1,0:T(8,128)}), f32[128,1024]{1,0:T(8,128)}) %reduce-scatter.15.cloned.1.call-update) | async-done | bytes 524304 | tf_op jit(solution)/shard_map/reduce_scatter | solution.py:374
  351.0 54.9 %reduce-scatter.17.cloned.1.call-done = f32[1024,128]{1,0:T(8,128)} async-done(((f32[1024,1024]{1,0:T(8,128)}), f32[1024,128]{1,0:T(8,128)}) %reduce-scatter.17.cloned.1.call-update) | async-done | bytes 524304 | tf_op jit(solution)/shard_map/reduce_scatter | solution.py:375
  (116 shorter events, 13.7 us)
Async XLA Ops:
  7.2 14.8 %copy-start.15 = (s32[2,128]{1,0:T(2,128)S(1)}, s32[2,128]{1,0:T(2,128)}, u32[]{:S(2)}) copy-start(s32[2,128]{1,0:T(2,128)} %param.14) | copy-start | bytes 3076
  7.2 16.8 %copy-start = (bf16[2,128,1024]{2,1,0:T(8,128)(2,1)S(1)}, bf16[2,128,1024]{2,1,0:T(8,128)(2,1)}, u32[]{:S(2)}) copy-start(bf16[2,128,1024]{2,1,0:T(8,128)(2,1)} %param.12) | copy-start | bytes 1572868
  7.2 17.2 %copy-start.14 = (f32[2,1024]{1,0:T(2,128)S(1)}, f32[2,1024]{1,0:T(2,128)}, u32[]{:S(2)}) copy-start(f32[2,1024]{1,0:T(2,128)} %param.22) | copy-start | bytes 24580
  7.2 17.2 %copy-start.10 = (f32[4,1024]{1,0:T(4,128)S(1)}, f32[4,1024]{1,0:T(4,128)}, u32[]{:S(2)}) copy-start(f32[4,1024]{1,0:T(4,128)} %param.23) | copy-start | bytes 49156
  7.2 31.1 %copy-start.18 = (f32[3,256]{1,0:T(4,128)S(1)}, f32[3,256]{1,0:T(4,128)}, u32[]{:S(2)}) copy-start(f32[3,256]{1,0:T(4,128)} %param.17) | copy-start | bytes 9220
  7.2 31.0 %all-gather.5.cloned.1.call-start = ((), (), s32[]{:S(2)}) async-start(), calls=%async_computation.6 | async-start | bytes 1769472 | tf_op jit(solution)/shard_map/all_gather | solution.py:117
  8.0 51.3 %reduce-scatter.19.cloned.1.call-start = ((), (), s32[]{:S(2)}) async-start(), calls=%async_computation.14 | async-start | bytes 393216
  21.9 26.8 %copy-start.4 = (bf16[2,128,256]{1,2,0:T(8,128)(2,1)}, bf16[2,128,256]{1,2,0:T(8,128)(2,1)S(1)}, u32[]{:S(2)}) copy-start(bf16[2,128,256]{1,2,0:T(8,128)(2,1)S(1)} %copy.58) | copy-start | bytes 393220
  24.4 16.0 %copy-start.7 = (f32[2,128]{1,0:T(2,128)}, f32[2,128]{1,0:T(2,128)S(1)}, u32[]{:S(2)}) copy-start(f32[2,128]{1,0:T(2,128)S(1)} %add_rsqrt_fusion) | copy-start | bytes 3076
  25.1 15.3 %copy-start.13 = (f32[1,1024]{1,0:T(1,128)}, f32[1,1024]{1,0:T(1,128)S(1)}, u32[]{:S(2)}) copy-start(f32[1,1024]{1,0:T(1,128)S(1)} %get-tuple-element.150) | copy-start | bytes 12292
  40.3 0.9 copy-start.3
  47.6 1.1 copy-start.6
  51.3 19.6 %reduce-scatter.9.cloned.1.call-start = ((), (), s32[]{:S(2)}) async-start(), calls=%async_computation.9 | async-start | bytes 393216 | tf_op jit(solution)/shard_map/reduce_scatter | solution.py:318
  53.6 48.1 %all-gather.7.cloned.1.call-start = ((), (), s32[]{:S(2)}) async-start(), calls=%async_computation.7 | async-start | bytes 2359296 | tf_op jit(solution)/shard_map/all_gather | solution.py:119
  54.1 77.3 %all-gather.9.cloned.1.call-start = ((), (), s32[]{:S(2)}) async-start(), calls=%async_computation.8 | async-start | bytes 2359296 | tf_op jit(solution)/shard_map/all_gather | solution.py:120
  54.7 152.8 %all-reduce.4.cloned.1.call-start = ((), (), s32[]{:S(2)}) async-start(), calls=%async_computation.15 | async-start | bytes 3145728 | tf_op jit(solution)/shard_map/psum | solution.py:215
  60.6 41.0 %copy-start.8 = (f32[2,128]{1,0:T(2,128)S(1)}, f32[2,128]{1,0:T(2,128)}, u32[]{:S(2)}) copy-start(f32[2,128]{1,0:T(2,128)} %copy-done.7) | copy-start | bytes 3076
  60.7 41.0 %copy-start.19 = (f32[1024]{0:T(1024)S(1)}, f32[1024]{0:T(1024)}, u32[]{:S(2)}) copy-start(f32[1024]{0:T(1024)} %param.20) | copy-start | bytes 12292
  104.0 30.0 %copy-start.5 = (bf16[2,128,4,64]{1,3,2,0:T(8,128)(2,1)S(1)}, bf16[2,128,4,64]{1,3,2,0:T(8,128)(2,1)}, u32[]{:S(2)}) copy-start(bf16[2,128,4,64]{1,3,2,0:T(8,128)(2,1)} %get-tuple-element.165) | copy-start | bytes 393220
  131.5 3.6 copy-start.2
  133.9 1.1 copy-start.1
  135.1 1.6 copy-start.17
  138.3 117.8 %reduce-scatter.11.cloned.1.call-start = ((), (), s32[]{:S(2)}) async-start(), calls=%async_computation.10 | async-start | bytes 3538944 | tf_op jit(solution)/shard_map/reduce_scatter | solution.py:372
  141.6 154.2 %reduce-scatter.13.cloned.1.call-start = ((), (), s32[]{:S(2)}) async-start(), calls=%async_computation.11 | async-start | bytes 1179648 | tf_op jit(solution)/shard_map/reduce_scatter | solution.py:373
  143.0 208.0 %reduce-scatter.15.cloned.1.call-start = ((), (), s32[]{:S(2)}) async-start(), calls=%async_computation.12 | async-start | bytes 4718592 | tf_op jit(solution)/shard_map/reduce_scatter | solution.py:374
  146.5 259.3 %reduce-scatter.17.cloned.1.call-start = ((), (), s32[]{:S(2)}) async-start(), calls=%async_computation.13 | async-start | bytes 4718592 | tf_op jit(solution)/shard_map/reduce_scatter | solution.py:375
  149.5 58.0 %copy-start.9 = (f32[2,128]{1,0:T(2,128)S(1)}, f32[2,128]{1,0:T(2,128)}, u32[]{:S(2)}) copy-start(f32[2,128]{1,0:T(2,128)} %copy-done.7) | copy-start | bytes 3076
  149.5 60.2 %copy-start.11 = (f32[1,1024]{1,0:T(1,128)S(1)}, f32[1,1024]{1,0:T(1,128)}, u32[]{:S(2)}) copy-start(f32[1,1024]{1,0:T(1,128)} %get-tuple-element.148) | copy-start | bytes 12292
  149.5 60.2 %copy-start.12 = (f32[1,1024]{1,0:T(1,128)S(1)}, f32[1,1024]{1,0:T(1,128)}, u32[]{:S(2)}) copy-start(f32[1,1024]{1,0:T(1,128)} %get-tuple-element.151) | copy-start | bytes 12292
  209.7 3.4 copy-start.16
Sparse Core Ops, SparseCore 0:
  9.9 28.2 all-gather.4
  51.5 7.7 reduce-scatter.18
  62.0 8.8 reduce-scatter.8
  72.7 28.8 all-gather.6
  103.3 28.0 all-gather.8
  138.4 69.0 all-reduce.3
  210.9 45.1 reduce-scatter.10
  259.8 35.9 reduce-scatter.12
  299.8 51.1 reduce-scatter.14
  354.7 51.0 reduce-scatter.16
where the time goes:
time: 413 us
  waiting for transfers between devices  308 us (75%)
  blocking collectives  41.8 us (10%)
  matrix products  30.9 us (7%)
  between operations  14.7 us (4%)
  other arithmetic  8.64 us (2%)
  local copies, waits for them, and re-layouts  8.09 us (2%)
    psum x1, waiting for transfers between devices, shards(): lax.psum(partial_output_sum.astype(jnp.bfloat16), 'tensor')  57.9 us
    reduce_scatter x1, waiting for transfers between devices, shards(): lax.psum_scatter(grad_fc1_w, ('dp', 'seq'), scatter_dimension=0, tiled=True)  55.1 us
    reduce_scatter x1, waiting for transfers between devices, shards(): lax.psum_scatter(gradient_down_weight, ('dp', 'seq'), scatter_dimension=1...  54.9 us
    reduce_scatter x1, waiting for transfers between devices, shards(): lax.psum_scatter(gradient_output_weight, ('dp', 'seq'), scatter_dimension...  37.8 us
    all_gather x1, waiting for transfers between devices, shards(): lax.all_gather(w_fc2, ('dp', 'seq'), axis=1, tiled=True)  27.5 us
    all_gather x1, waiting for transfers between devices, shards(): lax.all_gather(w_fc1, ('dp', 'seq'), axis=0, tiled=True)  26.9 us
    psum x1, blocking collectives, shards(): lax.psum((grad_bias_qkv, jnp.sum(grad_pre, axis=(0, 1)), gain_terms, row_...  24.2 us
    reduce_scatter x1, waiting for transfers between devices, shards(): lax.psum_scatter(grad_qkv_w, ('dp', 'seq'), scatter_dimension=1, tiled=True)  18.7 us
  transfers between devices with their start and end apart: 10, of which 10 were waited for; matrix products, arithmetic and copies ran while one was open for 8% of the time, Pallas kernels for 0%

commit v1 on v0

--- a/solution.py
+++ b/solution.py
@@ -1,8 +1,11 @@
+import functools
 import math
 
 import jax
 import jax.numpy as jnp
 from jax import lax
+from jax.experimental import pallas as pl
+from jax.experimental.pallas import tpu as pltpu
 from jax.sharding import PartitionSpec as P
 
 HD = 64
@@ -388,9 +391,444 @@
     )
 
 
+MESH = pl.DeviceIdType.MESH
+ANY = pl.BlockSpec(memory_space=pl.ANY)
+VM = pl.BlockSpec(memory_space=pltpu.VMEM)
+
+
+def shard_views(refs, index, sizes):
+    spans = [pl.ds(pl.multiple_of(index * n, n), n) for n in sizes]
+    return (
+        refs[0].at[:, spans[0], :],
+        refs[1].at[:, spans[1]],
+        refs[2].at[spans[2], :],
+        refs[3].at[:, spans[3]],
+    )
+
+
+def remote(src, dst, send, recv, where):
+    return pltpu.make_async_remote_copy(
+        src_ref=src, dst_ref=dst, send_sem=send, recv_sem=recv, device_id=where, device_id_type=MESH
+    )
+
+
+def gather_kernel(ndp, sizes, *refs):
+    (wq, wo, w1, w2, x, c, sp, gq, go, g1, g2, gx, gc, gsp) = refs[:14]
+    send, recv, send2, recv2, local, psend, precv, plocal = refs[14:]
+    nseq = 2
+    d, s = lax.axis_index("dp"), lax.axis_index("seq")
+    other = 1 - s
+    shards_in = (wq, wo, w1, w2)
+    full = (gq, go, g1, g2)
+    pairs = ((x, gx), (c, gc), (sp, gsp))
+
+    barrier = pltpu.get_barrier_semaphore()
+    for k in range(1, ndp):
+        pl.semaphore_signal(barrier, inc=1, device_id={"dp": lax.rem(d + k, ndp)}, device_id_type=MESH)
+    pl.semaphore_signal(barrier, inc=1, device_id={"seq": other}, device_id_type=MESH)
+    pl.semaphore_wait(barrier, ndp)
+
+    mine = shard_views(full, d * nseq + s, sizes)
+    far = []
+    near = []
+    for a in range(4):
+        for k in range(1, ndp):
+            copy = remote(
+                shards_in[a], mine[a], send.at[a, k], recv.at[a, k], {"dp": lax.rem(d + k, ndp)}
+            )
+            copy.start()
+            far.append((a, k, copy))
+    for j, (src, dst) in enumerate(pairs):
+        copy = remote(src, dst.at[:, s], psend.at[j], precv.at[j], {"seq": other})
+        copy.start()
+        near.append(copy)
+    here = []
+    for j, (src, dst) in enumerate(pairs):
+        copy = pltpu.make_async_copy(src, dst.at[:, s], plocal.at[j])
+        copy.start()
+        here.append(copy)
+    for a in range(4):
+        copy = remote(shards_in[a], mine[a], send2.at[a, 0], recv2.at[a, 0], {"seq": other})
+        copy.start()
+        near.append(copy)
+        copy = pltpu.make_async_copy(shards_in[a], mine[a], local.at[a])
+        copy.start()
+        here.append(copy)
+    for a, k, copy in far:
+        copy.wait_recv()
+        view = shard_views(full, lax.rem(d + ndp - k, ndp) * nseq + s, sizes)[a]
+        onward = remote(view, view, send2.at[a, k], recv2.at[a, k], {"seq": other})
+        onward.start()
+        near.append(onward)
+    for copy in here:
+        copy.wait()
+    for _, _, copy in far:
+        copy.wait_send()
+    for copy in near:
+        copy.wait()
+
+
+def reduce_kernel(ndp, nt, sizes, *refs):
+    (pq, po, p1, p2, zin, bin_) = refs[:6]
+    (oq, oo, o1, o2, zout, bout) = refs[6:12]
+    own = refs[12:16]
+    got1 = refs[16:20]
+    got2 = refs[20:24]
+    zgot, bpair, bsum, bgot2, bsum2, bgot3 = refs[24:30]
+    (s1, r1, l1, s2, r2, zs, zr, as_, ar, b1s, b1r, b2s, b2r, b3s, b3r) = refs[30:]
+    nseq = 2
+    partial = (pq, po, p1, p2)
+    outs = (oq, oo, o1, o2)
+    d, s, t = lax.axis_index("dp"), lax.axis_index("seq"), lax.axis_index("tensor")
+    other = 1 - s
+    rows = zin.shape[1] // nt
+
+    barrier = pltpu.get_barrier_semaphore()
+    for k in range(1, ndp):
+        pl.semaphore_signal(barrier, inc=1, device_id={"dp": lax.rem(d + k, ndp)}, device_id_type=MESH)
+    for k in range(1, nt):
+        pl.semaphore_signal(
+            barrier, inc=1, device_id={"tensor": lax.rem(t + k, nt)}, device_id_type=MESH
+        )
+    pl.semaphore_signal(barrier, inc=1, device_id={"seq": other}, device_id_type=MESH)
+    pl.semaphore_wait(barrier, ndp + nt - 1)
+
+    def band(index):
+        return pl.ds(pl.multiple_of(index * rows, rows), rows)
+
+    zsends = []
+    for k in range(1, nt):
+        peer = lax.rem(t + k, nt)
+        copy = remote(zin.at[:, band(peer)], zgot.at[k], zs.at[k], zr.at[k], {"tensor": peer})
+        copy.start()
+        zsends.append(copy)
+    first = {}
+    mine = {}
+    order = list(range(1, ndp)) + [0]
+    for k in order:
+        dest = lax.rem(d + k, ndp)
+        give = shard_views(partial, dest * nseq + other, sizes)
+        keep = shard_views(partial, dest * nseq + s, sizes)
+        for a in range(4):
+            copy = remote(give[a], got1[a].at[k], s1.at[a, k], r1.at[a, k], {"seq": other})
+            copy.start()
+            first[a, k] = copy
+            copy = pltpu.make_async_copy(keep[a], own[a].at[k], l1.at[a, k])
+            copy.start()
+            mine[a, k] = copy
+    bpair_copy = remote(bin_, bpair, b1s, b1r, {"seq": other})
+    bpair_copy.start()
+
+    second = {}
+    for k in order:
+        for a in range(4):
+            mine[a, k].wait()
+            first[a, k].wait_recv()
+            own[a][k] = (
+                own[a][k].astype(jnp.float32) + got1[a][k].astype(jnp.float32)
+            ).astype(own[a].dtype)
+            if k:
+                copy = remote(
+                    own[a].at[k], got2[a].at[k], s2.at[a, k], r2.at[a, k], {"dp": lax.rem(d + k, ndp)}
+                )
+                copy.start()
+                second[a, k] = copy
+
+    bpair_copy.wait()
+    bsum[...] = bin_[...] + bpair[...]
+    bsends = []
+    for k in range(1, ndp):
+        copy = remote(bsum, bgot2.at[d], b2s.at[k], b2r.at[k], {"dp": lax.rem(d + k, ndp)})
+        copy.start()
+        bsends.append(copy)
+
+    total = zin[:, band(t)].astype(jnp.float32)
+    for k, copy in zip(range(1, nt), zsends):
+        copy.wait_recv()
+        total = total + zgot[k].astype(jnp.float32)
+    zout[:, band(t)] = total.astype(zout.dtype)
+    asends = []
+    for k in range(1, nt):
+        peer = lax.rem(t + k, nt)
+        copy = remote(
+            zout.at[:, band(t)], zout.at[:, band(t)], as_.at[k], ar.at[k], {"tensor": peer}
+        )
+        copy.start()
+        asends.append(copy)
+
+    for copy in bsends:
+        copy.wait()
+    bgot2[d] = bsum[...]
+    plane = bgot2[0]
+    for k in range(1, ndp):
+        plane = plane + bgot2[k]
+    bsum2[...] = plane
+    bsends = []
+    for k in range(1, nt):
+        copy = remote(bsum2, bgot3.at[t], b3s.at[k], b3r.at[k], {"tensor": lax.rem(t + k, nt)})
+        copy.start()
+        bsends.append(copy)
+
+    for a in range(4):
+        acc = own[a][0].astype(jnp.float32)
+        for k in range(1, ndp):
+            second[a, k].wait_recv()
+            acc = acc + got2[a][k].astype(jnp.float32)
+        outs[a][...] = acc
+
+    for copy in bsends:
+        copy.wait()
+    bgot3[t] = bsum2[...]
+    whole = bgot3[0]
+    for k in range(1, nt):
+        whole = whole + bgot3[k]
+    bout[0] = bsum2[...]
+    bout[1] = whole
+    for copy in asends:
+        copy.wait()
+    for copy in zsends:
+        copy.wait_send()
+    for copy in first.values():
+        copy.wait_send()
+    for copy in second.values():
+        copy.wait_send()
+
+
+def gather_all(ndp, sizes, w_qkv, w_out, w_fc1, w_fc2, tokens, cotangent, ids):
+    shape = jax.ShapeDtypeStruct
+    many = ndp * 2
+    seqs, rows, width = tokens.shape
+    dma = pltpu.SemaphoreType.DMA
+    return pl.pallas_call(
+        functools.partial(gather_kernel, ndp, sizes),
+        out_shape=(
+            shape((w_qkv.shape[0], w_qkv.shape[1] * many, w_qkv.shape[2]), w_qkv.dtype),
+            shape((w_out.shape[0], w_out.shape[1] * many), w_out.dtype),
+            shape((w_fc1.shape[0] * many, w_fc1.shape[1]), w_fc1.dtype),
+            shape((w_fc2.shape[0], w_fc2.shape[1] * many), w_fc2.dtype),
+            shape((seqs, 2, rows, width), tokens.dtype),
+            shape((seqs, 2, rows, width), cotangent.dtype),
+            shape((ids.shape[0], 2) + ids.shape[1:], ids.dtype),
+        ),
+        in_specs=[VM] * 7,
+        out_specs=[ANY] * 7,
+        scratch_shapes=[
+            dma((4, ndp)),
+            dma((4, ndp)),
+            dma((4, ndp)),
+            dma((4, ndp)),
+            dma((4,)),
+            dma((3,)),
+            dma((3,)),
+            dma((3,)),
+        ],
+        compiler_params=pltpu.CompilerParams(collective_id=0, has_side_effects=True),
+    )(w_qkv, w_out, w_fc1, w_fc2, tokens, cotangent, ids)
+
+
+def reduce_all(ndp, nt, sizes, partials, zin, bias_rows):
+    shape = jax.ShapeDtypeStruct
+    many = ndp * 2
+    pq, po, p1, p2 = partials
+    dma = pltpu.SemaphoreType.DMA
+    shards_shape = (
+        (pq.shape[0], pq.shape[1] // many, pq.shape[2]),
+        (po.shape[0], po.shape[1] // many),
+        (p1.shape[0] // many, p1.shape[1]),
+        (p2.shape[0], p2.shape[1] // many),
+    )
+    stacks = [pltpu.VMEM((ndp,) + part, jnp.bfloat16) for part in shards_shape]
+    rows = zin.shape[1] // nt
+    bias_shape = bias_rows.shape
+    return pl.pallas_call(
+        functools.partial(reduce_kernel, ndp, nt, sizes),
+        out_shape=tuple(shape(part, jnp.float32) for part in shards_shape)
+        + (shape(zin.shape, zin.dtype), shape((2,) + bias_shape, jnp.float32)),
+        in_specs=[ANY] * 4 + [VM] * 2,
+        out_specs=[VM] * 6,
+        scratch_shapes=stacks
+        + stacks
+        + stacks
+        + [
+            pltpu.VMEM((nt, zin.shape[0], rows, zin.shape[2]), zin.dtype),
+            pltpu.VMEM(bias_shape, jnp.float32),
+            pltpu.VMEM(bias_shape, jnp.float32),
+            pltpu.VMEM((ndp,) + bias_shape, jnp.float32),
+            pltpu.VMEM(bias_shape, jnp.float32),
+            pltpu.VMEM((nt,) + bias_shape, jnp.float32),
+            dma((4, ndp)),
+            dma((4, ndp)),
+            dma((4, ndp)),
+            dma((4, ndp)),
+            dma((4, ndp)),
+            dma((nt,)),
+            dma((nt,)),
+            dma((nt,)),
+            dma((nt,)),
+            dma,
+            dma,
+            dma((ndp,)),
+            dma((ndp,)),
+            dma((nt,)),
+            dma((nt,)),
+        ],
+        compiler_params=pltpu.CompilerParams(collective_id=1, has_side_effects=True),
+    )(pq, po, p1, p2, zin, bias_rows)
+
+
+def block(mesh, *args):
+    seqs, rows, _ = args[0].shape
+    heads = args[4].shape[2] // HD
+    length = rows * mesh.shape["seq"]
+    if mesh.shape["seq"] == 2 and seqs * heads * length * length * 4 <= 2**23:
+        return whole_rows(mesh.shape["dp"], mesh.shape["tensor"], *args)
+    return shards(*args)
+
+
+def whole_rows(
+    ndp,
+    nt,
+    block_input,
+    cotangent,
+    segments,
+    positions,
+    w_qkv,
+    qkv_bias,
+    w_out,
+    w_fc1,
+    fc1_bias,
+    w_fc2,
+    ln_gains,
+    row_biases,
+):
+    seqs, rows, width = block_input.shape
+    length = rows * 2
+    heads = w_qkv.shape[2] // HD
+    flat = heads * HD
+    scale = HD ** (-0.5)
+    f32, bf16 = jnp.float32, jnp.bfloat16
+    sizes = (w_qkv.shape[1], w_out.shape[1], w_fc1.shape[0], w_fc2.shape[1])
+    ids = jnp.stack([segments, positions], axis=1)
+    wq, wo, w1, w2, xg, cg, idg = gather_all(
+        ndp, sizes, w_qkv, w_out, w_fc1, w_fc2, block_input, cotangent, ids
+    )
+    x_all = xg.reshape(seqs, length, width)
+    c_all = cg.reshape(seqs, length, width)
+    seg = idg[:, :, 0].reshape(seqs, length)
+    pos = idg[:, :, 1].reshape(seqs, length)
+    start = lax.axis_index("seq") * rows
+
+    def here(array):
+        return lax.dynamic_slice_in_dim(array, start, rows, array.ndim - 2)
+
+    first_all = layer_norm(x_all.astype(f32), ln_gains[0], row_biases[0])[0].astype(bf16)
+    inputs_f = block_input.astype(f32)
+    second_out, normed, inv_std = layer_norm(inputs_f, ln_gains[1], row_biases[1])
+    second = second_out.astype(bf16)
+    first = (normed * ln_gains[0] + row_biases[0]).astype(bf16)
+
+    projected = (
+        jnp.einsum("bxf,kfh->kbxh", first_all, wq, preferred_element_type=f32)
+        + qkv_bias[:, None, None, :]
+    )
+    shape_heads = (seqs, length, heads, HD)
+    cosine, sine = rotary_tables(pos)
+    queries = rotate(projected[0].reshape(shape_heads), cosine, sine).astype(bf16)
+    keys = rotate(projected[1].reshape(shape_heads), cosine, sine).astype(bf16)
+    values = projected[2].reshape(shape_heads).astype(bf16)
+    token = jnp.arange(length)
+    allowed = (
+        (seg[:, :, None] == seg[:, None, :]) & (token[None, None, :] <= token[None, :, None])
+    )[:, None]
+    scores = jnp.einsum("sqhd,skhd->shqk", queries, keys, preferred_element_type=f32) * scale
+    row_max = jnp.max(jnp.where(allowed, scores, neg_big), axis=-1, keepdims=True)
+    expo = jnp.where(allowed, jnp.exp(scores - row_max), 0.0)
+    row_sum = jnp.sum(expo, axis=-1, keepdims=True)
+    mixed = jnp.einsum("shqk,skhd->shqd", expo.astype(bf16), values, preferred_element_type=f32)
+    context = (mixed / row_sum).transpose(0, 2, 1, 3).reshape(seqs, length, flat).astype(bf16)
+    grad_context = jnp.einsum("sli,zi->slz", c_all, wo, preferred_element_type=f32).astype(bf16)
+    grad_ctx_heads = grad_context.reshape(shape_heads)
+    delta = jnp.sum(
+        grad_ctx_heads.astype(f32) * context.reshape(shape_heads).astype(f32), axis=-1
+    ).transpose(0, 2, 1)
+    probs = expo / row_sum
+    grad_p = jnp.einsum("sqhd,skhd->shqk", grad_ctx_heads, values, preferred_element_type=f32)
+    grad_s = (probs * (grad_p - delta[..., None])).astype(bf16)
+    grad_v = jnp.einsum(
+        "shqk,sqhd->skhd", probs.astype(bf16), grad_ctx_heads, preferred_element_type=f32
+    )
+    grad_q = jnp.einsum("shqk,skhd->sqhd", grad_s, keys, preferred_element_type=f32) * scale
+    grad_k = jnp.einsum("shqk,sqhd->skhd", grad_s, queries, preferred_element_type=f32) * scale
+    grad_proj = jnp.stack(
+        [
+            here(unrotate(grad_q, cosine, sine).reshape(seqs, length, flat)),
+            here(unrotate(grad_k, cosine, sine).reshape(seqs, length, flat)),
+            here(grad_v.reshape(seqs, length, flat)),
+        ]
+    )
+    context_here = here(context)
+    grad_bias_qkv = jnp.sum(grad_proj, axis=(1, 2))
+    grad_proj_in = grad_proj.astype(bf16)
+
+    pre_act = jnp.einsum("vrk,kt->vrt", second, w1, preferred_element_type=f32) + fc1_bias
+    activ, gelu_slope = gelu_pair(pre_act)
+    hidden = activ.astype(bf16)
+    branches = jnp.einsum("qhw,wj->qhj", context_here, wo, preferred_element_type=f32) + jnp.einsum(
+        "qzg,gc->qzc", hidden, w2, preferred_element_type=f32
+    )
+    grad_f = cotangent.astype(f32)
+    grad_pre = jnp.einsum("hvg,rg->hvr", cotangent, w2, preferred_element_type=f32) * gelu_slope
+    grad_hidden = grad_pre.astype(bf16)
+    grad_second = jnp.einsum("ikq,uq->iku", grad_hidden, w1, preferred_element_type=f32)
+    grad_first = jnp.einsum("etbp,eop->tbo", grad_proj_in, wq, preferred_element_type=f32)
+    partials = (
+        jnp.einsum("ink,oint->okt", first, grad_proj_in, preferred_element_type=f32).astype(bf16),
+        jnp.einsum("bxz,bxe->ze", context_here, cotangent, preferred_element_type=f32).astype(bf16),
+        jnp.einsum("mxa,mxr->ar", second, grad_hidden, preferred_element_type=f32).astype(bf16),
+        jnp.einsum("tzi,tzo->io", hidden, cotangent, preferred_element_type=f32).astype(bf16),
+    )
+    scaled = grad_first * ln_gains[0] + grad_second * ln_gains[1]
+    hid = w_fc1.shape[1]
+    wide = max(width, hid, qkv_bias.size)
+    line = lambda v: jnp.pad(v.reshape(-1), (0, wide - v.size))
+    bias_rows = jnp.stack(
+        [
+            line(jnp.sum(grad_pre, axis=(0, 1))),
+            line(grad_bias_qkv),
+            line(jnp.sum(grad_first * normed, axis=(0, 1))),
+            line(jnp.sum(grad_second * normed, axis=(0, 1))),
+            line(jnp.sum(grad_first, axis=(0, 1))),
+            line(jnp.sum(grad_second, axis=(0, 1))),
+            line(jnp.sum(grad_f, axis=(0, 1))),
+            jnp.zeros((wide,), f32),
+        ]
+    )
+    zin = jnp.stack([branches, scaled]).astype(bf16).reshape(2, seqs * rows, width)
+    gq, go, g1, g2, zsum, bias = reduce_all(ndp, nt, sizes, partials, zin, bias_rows)
+    zsum = zsum.astype(f32).reshape(2, seqs, rows, width)
+    output = (inputs_f + zsum[0] + row_biases[2] + row_biases[3]).astype(bf16)
+    centre = jnp.mean(zsum[1], axis=-1, keepdims=True)
+    slope = jnp.mean(zsum[1] * normed, axis=-1, keepdims=True)
+    grad_input = grad_f + inv_std * (zsum[1] - centre - normed * slope)
+    total = bias[1, :, :width]
+    grad_ct = bias[0, 6, :width]
+    return (
+        output,
+        grad_input,
+        gq,
+        go,
+        g1,
+        g2,
+        bias[0, 1, : qkv_bias.size].reshape(qkv_bias.shape),
+        bias[0, 0, :hid],
+        total[2:4],
+        jnp.stack([total[4], total[5], grad_ct, grad_ct]),
+    )
+
+
 def solution(mesh):
     return jax.shard_map(
-        shards,
+        functools.partial(block, mesh),
         mesh=mesh,
         in_specs=(
             P("dp", "seq", None),

time: 413 us -> 148 us (0.36)
  waiting for transfers between devices: 308 us -> 0 us
  Pallas kernels: 0 us -> 99.6 us
  blocking collectives: 41.8 us -> 0 us
  between operations: 14.7 us -> 1.27 us
  matrix products: 30.9 us -> 21.9 us
  local copies, waits for them, and re-layouts: 8.09 us -> 14.3 us
    reduce_scatter x5 -> x0, waiting for transfers between devices: 177 us -> none  [the longest x1 55.1 us: shards(): lax.psum_scatter(grad_fc1_w, ('dp', 'seq'), scatter_dimension=0, tiled=True)]
    pallas_call x0 -> x2, Pallas kernels: none -> 99.6 us  [the longest x1 56.9 us: reduce_all(): pl.pallas_call(functools.partial(reduce_kernel, ndp, nt, sizes), out_shap...]
    all_gather x3 -> x0, waiting for transfers between devices: 67.4 us -> none  [the longest x1 27.5 us: shards(): lax.all_gather(w_fc2, ('dp', 'seq'), axis=1, tiled=True)]
    psum x1 -> x0, waiting for transfers between devices: 57.9 us -> none  [shards(): lax.psum(partial_output_sum.astype(jnp.bfloat16), 'tensor')]
    psum x1 -> x0, blocking collectives: 24.2 us -> none  [shards(): lax.psum((grad_bias_qkv, jnp.sum(grad_pre, axis=(0, 1)), gain_terms, row_...]
    all_gather x4 -> x0, blocking collectives: 17.6 us -> none  [the longest x1 11.7 us: shards(): lax.all_gather(w_out, ('dp', 'seq'), axis=1, tiled=True)]
    dot_general x18 -> x17, matrix products: 30.9 us -> 20.8 us  [the longest x1 2.37 us: whole_rows(): jnp.einsum('qzg,gc->qzc', hidden, w2, preferred_element_type=f32)]
    unnamed x11 -> x0, waiting for transfers between devices: 6 us -> none
  transfers between devices with their start and end apart: 10 -> 0, of which waited for: 10 -> 0; matrix products, arithmetic and copies ran while one was open for 8% -> 0% of each run, Pallas kernels for 0% -> 0%
where the time goes in v1:
time: 148 us; the launch traced here: 147 us
  Pallas kernels  99.6 us (67%)
  matrix products  21.9 us (15%)
  local copies, waits for them, and re-layouts  14.3 us (10%)
  other arithmetic  10.3 us (7%)
    pallas_call x1, Pallas kernels, reduce_all(): pl.pallas_call(functools.partial(reduce_kernel, ndp, nt, sizes), out_shap...  56.9 us
    pallas_call x1, Pallas kernels, gather_all(): pl.pallas_call(functools.partial(gather_kernel, ndp, sizes), out_shape=(s...  42.7 us
    unnamed x58, local copies, waits for them, and re-layouts  6.12 us

profile of v1, /device:TPU:0, one launch (start us, length us, event | category | flops | bytes accessed | tf_op | source)
XLA Modules:
  0.0 147.4 jit_solution(9915586866755943038)
XLA Ops:
  0.7 1.3 pad_add_fusion.refs_6_
  2.0 42.7 %shard_map.195 = (bf16[3,1024,256]{2,1,0:T(8,128)(2,1)}, bf16[256,1024]{1,0:T(8,128)(2,1)}, bf16[1024,1024]{1,0:T(8,128)(2,1)}, bf16[1024,1024]{1,0:T(8,128)(2,1...) custom-call(bf16[3,128,256]{2,1,0:T(8,128)(2,1)} %refs_0_.1, ...), custom_call_target="tpu_custom_call" | custom-call | tf_op jit(solution)/shard_map/pallas_call | solution.py:602
  44.7 1.6 %convert_reduce_fusion.2 = f32[2,2,128]{2,1,0:T(2,128)S(1)} fusion(bf16[2,2,128,1024]{3,2,1,0:T(8,128)(2,1)} %get-tuple-element.24), kind=kLoop, calls=%fused_computation.77 | loop fusion | flops 1048064 | bytes 1050624 | tf_op jit(solution)/shard_map/reduce_sum | solution.py:22
  46.3 1.6 %multiply_reduce_fusion = f32[2,2,128]{2,1,0:T(2,128)S(1)} fusion(bf16[2,2,128,1024]{3,2,1,0:T(8,128)(2,1)} %get-tuple-element.24, f32[2,2,128]{2,1,0:T(2,128)S(1)} %get-tuple-element.76), kind=kLoop, calls=%fused_computation.21 | loop fusion | flops 2096640 | bytes 1052672 | tf_op jit(solution)/shard_map/reduce_sum | solution.py:23
  48.5 1.0 add_bitcast_fusion
  51.0 1.1 fusion.117
  52.1 1.4 slice.221
  53.6 1.7 %convolution_convert_fusion = bf16[2,256,256]{1,2,0:T(8,128)(2,1)S(1)} fusion(bf16[2,256,1024]{2,1,0:T(8,128)(2,1)} %bitcast.213, bf16[256,1024]{1,0:T(8,128)(2,1)S(1)} %copy-done.10), kind=kOutput, calls=%fused_computation.58 | convolution fusion | flops 268566528 | bytes 1835008 | tf_op jit(solution)/shard_map/sli,zi->slz/dot_general | solution.py:749
  55.3 1.0 multiply_reduce_fusion.1
  58.0 0.7 copy-done.16
  58.7 2.2 %fusion.67 = f32[2,4,64,256]{3,2,1,0:T(8,128)S(1)} fusion(bf16[2,256,4,64]{1,3,2,0:T(8,128)(2,1)S(1)} %bitcast.183, f32[2,4,256,256]{2,3,1,0:T(8,128)} %copy-done.5, f32[2,4,256]{2,1,0:T(4,128)S(1)} %get-tuple-element.77), kind=kOutput, calls=%fused_computation.81 | convolution fusion | flops 68157440 | bytes 2891776 | tf_op jit(solution)/shard_map/shqk,sqhd->skhd/dot_general | solution.py:757
  62.8 0.8 fusion.33
  63.8 0.7 copy-done.4
  64.6 1.0 fusion.118
  65.6 1.0 fusion.109
  66.7 0.7 stack.74.refs_5_
  67.4 2.4 %fusion.5 = f32[2,128,1024]{2,1,0:T(8,128)S(1)} fusion(bf16[1024,1024]{1,0:T(8,128)(2,1)} %get-tuple-element.28, f32[2,128,1024]{2,1,0:T(8,128)S(1)} %fusion.33), kind=kOutput, calls=%fused_computation.8 | convolution fusion | flops 538181632 | bytes 4194304 | tf_op jit(solution)/shard_map/qzg,gc->qzc/dot_general | solution.py:776
  70.1 1.1 pad_maximum_fusion.refs_4_
  71.2 1.9 %fusion.21.refs_0_ = bf16[3,1024,256]{2,1,0:T(8,128)(2,1)} fusion(bf16[2,128,1024]{2,1,0:T(8,128)(2,1)S(1)} %copy-done.1, f32[1024]{0:T(1024)S(1)} %bitcast.191, f32[1024]{0:T(1024)S(1)} %bitcast.189, f32[2,128]{1,0:T(2,128)S(1)} %add_rsqrt_fusion, f32[2,128]{1,0:T(2,128)S(1)} %broadcast_multiply_fusion.2, ...), kind=kOutput, calls=%fused_computation.32 | convolution fusion | flops 405405696 | bytes 2893824 | tf_op jit(solution)/shard_map/ink,oint->okt/dot_general | solution.py:785
  73.2 1.3 fusion.36.refs_1_
  74.4 2.2 %bitcast_convert_fusion.1.refs_2_ = bf16[1024,1024]{1,0:T(8,128)(2,1)} fusion(bf16[2,128,1024]{2,1,0:T(8,128)(2,1)S(1)} %copy-done.1, f32[1024]{0:T(1024)S(1)} %bitcast.209, f32[1024]{0:T(1024)S(1)} %bitcast.207, f32[2,128]{1,0:T(2,128)S(1)} %add_rsqrt_fusion, f32[2,128]{1,0:T(2,128)S(1)} %broadcast_multiply_fusion.2, bf16[2,128,1024]{2,1,0:T(8,128)(2,1)S(1)} %copy-done.25), kind=kOutput, calls=%fused_computation.2 | convolution fusion | flops 539492352 | bytes 3155968 | tf_op jit(solution)/shard_map/mxa,mxr->ar/dot_general | solution.py:787
  76.7 2.1 %bitcast_convert_fusion.refs_3_ = bf16[1024,1024]{1,0:T(8,128)(2,1)} fusion(bf16[2,128,1024]{2,1,0:T(8,128)(2,1)S(1)} %copy-done, f32[2,128,1024]{2,1,0:T(8,128)S(1)} %fusion.33), kind=kOutput, calls=%fused_computation.1 | convolution fusion | flops 539230208 | bytes 3670016 | tf_op jit(solution)/shard_map/tzi,tzo->io/dot_general | solution.py:788
  78.7 56.9 %shard_map.196 = (f32[3,128,256]{2,1,0:T(8,128)}, f32[256,128]{1,0:T(8,128)}, f32[128,1024]{1,0:T(8,128)}, f32[1024,128]{1,0:T(8,128)}, bf16[2,256,1024]{2,1,0:T(8,128)(2,1)}, /*index=5*/f32[2,8,1024]{2,1,0:T(8,128)}) custom-call(bf16[3,1024,256]{2,1,0:T(8,128)(2,1)} %fusion.21.refs_0_, bf16[256,1024]{1,0:T(8,128)(2,1)} %fusion.36.refs_1_, ...), custom_call_target="tpu_custom_call" | custom-call | tf_op jit(solution)/shard_map/pallas_call | solution.py:643
  135.7 1.4 slice_bitcast_fusion.3
  137.7 1.5 %fusion.112 = (f32[1,256,1024]{2,1,0:T(8,128)S(1)}, f32[1,256,1024]{2,1,0:T(8,128)S(1)}) fusion(bf16[2,256,1024]{2,1,0:T(8,128)(2,1)} %get-tuple-element.30), kind=kLoop, calls=%fused_computation.170 | loop fusion | bytes 4194304 | tf_op jit(solution)/shard_map/slice | solution.py:812
  140.0 1.6 %convert_add_fusion.1 = (f32[2,128,1024]{2,1,0:T(8,128)}, bf16[2,128,1024]{2,1,0:T(8,128)(2,1)}) fusion(bf16[2,128,1024]{2,1,0:T(8,128)(2,1)S(1)} %copy-done, bf16[2,128,1024]{2,1,0:T(8,128)(2,1)S(1)} %copy-done.1, f32[2,128,1024]{2,1,0:T(8,128)S(1)} %bitcast.166, f32[2,128]{1,0:T(2,128)S(1)} %broadcast_multiply_fusion.1, ...), kind=kLoop, calls=%fused_computation.39 | loop fusion | flops 3407872 | bytes 4730880 | tf_op jit(solution)/shard_map/add | solution.py:812
  141.6 0.8 slice_reduce_fusion
  143.0 1.4 slice_bitcast_fusion
  144.4 0.7 copy.62
  145.1 0.7 copy.63
  145.8 0.8 copy.64
  146.6 0.8 copy.65
  (103 shorter events, 7.9 us)
Async XLA Ops:
  0.6 47.3 %copy-start.18 = (f32[4,1024]{1,0:T(4,128)S(1)}, f32[4,1024]{1,0:T(4,128)}, u32[]{:S(2)}) copy-start(f32[4,1024]{1,0:T(4,128)} %param.23) | copy-start | bytes 49156
  0.7 47.4 %copy-start.19 = (f32[2,1024]{1,0:T(2,128)S(1)}, f32[2,1024]{1,0:T(2,128)}, u32[]{:S(2)}) copy-start(f32[2,1024]{1,0:T(2,128)} %param.22) | copy-start | bytes 24580
  44.7 3.3 %copy-start.3 = (bf16[2,2,128,1024]{3,2,1,0:T(8,128)(2,1)S(1)}, bf16[2,2,128,1024]{3,2,1,0:T(8,128)(2,1)}, u32[]{:S(2)}) copy-start(bf16[2,2,128,1024]{3,2,1,0:T(8,128)(2,1)} %get-tuple-element.24) | copy-start | bytes 3145732
  44.7 3.8 %copy-start.6 = (bf16[3,1024,256]{2,1,0:T(8,128)(2,1)S(1)}, bf16[3,1024,256]{2,1,0:T(8,128)(2,1)}, u32[]{:S(2)}) copy-start(bf16[3,1024,256]{2,1,0:T(8,128)(2,1)} %get-tuple-element.23) | copy-start | bytes 4718596
  44.7 3.8 %copy-start.22 = (f32[3,256]{1,0:T(4,128)S(1)}, f32[3,256]{1,0:T(4,128)}, u32[]{:S(2)}) copy-start(f32[3,256]{1,0:T(4,128)} %param.17) | copy-start | bytes 9220
  49.6 1.2 copy-start.8
  49.6 0.7 copy-start.20
  51.0 2.6 %copy-start.10 = (bf16[256,1024]{1,0:T(8,128)(2,1)S(1)}, bf16[256,1024]{1,0:T(8,128)(2,1)}, u32[]{:S(2)}) copy-start(bf16[256,1024]{1,0:T(8,128)(2,1)} %get-tuple-element.27) | copy-start | bytes 1572868
  52.1 4.2 %copy-start.5 = (f32[2,4,256,256]{2,3,1,0:T(8,128)}, f32[2,4,256,256]{2,3,1,0:T(8,128)S(1)}, u32[]{:S(2)}) copy-start(f32[2,4,256,256]{2,3,1,0:T(8,128)S(1)} %get-tuple-element.78) | copy-start | bytes 6291460
  55.3 1.6 %copy-start.15 = (bf16[2,256,256]{1,2,0:T(8,128)(2,1)}, bf16[2,256,256]{1,2,0:T(8,128)(2,1)S(1)}, u32[]{:S(2)}) copy-start(bf16[2,256,256]{1,2,0:T(8,128)(2,1)S(1)} %convolution_convert_fusion) | copy-start | bytes 786436
  57.8 1.0 copy-start.16
  58.7 2.4 %copy-start.7 = (bf16[3,1024,256]{2,1,0:T(8,128)(2,1)S(1)}, bf16[3,1024,256]{2,1,0:T(8,128)(2,1)}, u32[]{:S(2)}) copy-start(bf16[3,1024,256]{2,1,0:T(8,128)(2,1)} %get-tuple-element.23) | copy-start | bytes 4718596
  60.9 1.0 copy-start.1
  61.2 1.6 %copy-start.21 = (bf16[1024,1024]{1,0:T(8,128)(2,1)S(1)}, bf16[1024,1024]{1,0:T(8,128)(2,1)}, u32[]{:S(2)}) copy-start(bf16[1024,1024]{1,0:T(8,128)(2,1)} %get-tuple-element.29) | copy-start | bytes 6291460
  61.2 1.6 %copy-start.23 = (f32[1024]{0:T(1024)S(1)}, f32[1024]{0:T(1024)}, u32[]{:S(2)}) copy-start(f32[1024]{0:T(1024)} %param.20) | copy-start | bytes 12292
  62.8 1.0 copy-start
  62.8 1.8 %copy-start.4 = (bf16[1024,1024]{1,0:T(8,128)(2,1)S(1)}, bf16[1024,1024]{1,0:T(8,128)(2,1)}, u32[]{:S(2)}) copy-start(bf16[1024,1024]{1,0:T(8,128)(2,1)} %get-tuple-element.28) | copy-start | bytes 6291460
  65.6 1.1 copy-start.24
  67.4 2.4 %copy-start.9 = (bf16[2,256,4,64]{1,3,2,0:T(8,128)(2,1)S(1)}, bf16[2,256,4,64]{1,3,2,0:T(8,128)(2,1)}, u32[]{:S(2)}) copy-start(bf16[2,256,4,64]{1,3,2,0:T(8,128)(2,1)} %get-tuple-element.80) | copy-start | bytes 786436
  67.4 2.4 %copy-start.11 = (bf16[256,1024]{1,0:T(8,128)(2,1)S(1)}, bf16[256,1024]{1,0:T(8,128)(2,1)}, u32[]{:S(2)}) copy-start(bf16[256,1024]{1,0:T(8,128)(2,1)} %get-tuple-element.27) | copy-start | bytes 1572868
  71.2 3.2 %copy-start.25 = (bf16[2,128,1024]{2,1,0:T(8,128)(2,1)S(1)}, bf16[2,128,1024]{2,1,0:T(8,128)(2,1)}, u32[]{:S(2)}) copy-start(bf16[2,128,1024]{2,1,0:T(8,128)(2,1)} %copy-done.24) | copy-start | bytes 1572868
  137.7 1.9 %copy-start.2 = (bf16[2,256,1024]{2,1,0:T(8,128)(2,1)S(1)}, bf16[2,256,1024]{2,1,0:T(8,128)(2,1)}, u32[]{:S(2)}) copy-start(bf16[2,256,1024]{2,1,0:T(8,128)(2,1)} %get-tuple-element.30) | copy-start | bytes 3145732
  140.0 4.4 %copy-start.14 = (f32[3,128,256]{2,1,0:T(8,128)S(1)}, f32[3,128,256]{2,1,0:T(8,128)}, u32[]{:S(2)}) copy-start(f32[3,128,256]{2,1,0:T(8,128)} %get-tuple-element.101) | copy-start | bytes 1179652
  140.0 5.1 %copy-start.17 = (f32[256,128]{1,0:T(8,128)S(1)}, f32[256,128]{1,0:T(8,128)}, u32[]{:S(2)}) copy-start(f32[256,128]{1,0:T(8,128)} %get-tuple-element.102) | copy-start | bytes 393220
  140.0 5.8 %copy-start.13 = (f32[128,1024]{1,0:T(8,128)S(1)}, f32[128,1024]{1,0:T(8,128)}, u32[]{:S(2)}) copy-start(f32[128,1024]{1,0:T(8,128)} %get-tuple-element.103) | copy-start | bytes 1572868
  141.6 5.0 %copy-start.12 = (f32[1024,128]{1,0:T(8,128)S(1)}, f32[1024,128]{1,0:T(8,128)}, u32[]{:S(2)}) copy-start(f32[1024,128]{1,0:T(8,128)} %get-tuple-element.104) | copy-start | bytes 1572868

commit v2 on v1

--- a/solution.py
+++ b/solution.py
@@ -396,96 +396,129 @@
 VM = pl.BlockSpec(memory_space=pltpu.VMEM)
 
 
-def shard_views(refs, index, sizes):
+def remote(src, dst, send, recv, where):
+    return pltpu.make_async_remote_copy(
+        src_ref=src, dst_ref=dst, send_sem=send, recv_sem=recv, device_id=where, device_id_type=MESH
+    )
+
+
+def slots(n):
+    return ((0, False), (1, True), (2, True), (3, False), (4, False), (5, True))[:n]
+
+
+def pieces(refs, index, sizes):
     spans = [pl.ds(pl.multiple_of(index * n, n), n) for n in sizes]
     return (
-        refs[0].at[:, spans[0], :],
+        refs[0].at[0, spans[0], :],
+        refs[0].at[1, spans[0], :],
+        refs[0].at[2, spans[0], :],
         refs[1].at[:, spans[1]],
         refs[2].at[spans[2], :],
         refs[3].at[:, spans[3]],
     )
 
 
-def remote(src, dst, send, recv, where):
-    return pltpu.make_async_remote_copy(
-        src_ref=src, dst_ref=dst, send_sem=send, recv_sem=recv, device_id=where, device_id_type=MESH
-    )
-
-
-def gather_kernel(ndp, sizes, *refs):
+def plane_peers(d):
+    return d + 1 - 2 * lax.rem(d, 2), lax.rem(d + 2, 4), 3 - d
+
+
+def gather_kernel(sizes, *refs):
     (wq, wo, w1, w2, x, c, sp, gq, go, g1, g2, gx, gc, gsp) = refs[:14]
     send, recv, send2, recv2, local, psend, precv, plocal = refs[14:]
     nseq = 2
     d, s = lax.axis_index("dp"), lax.axis_index("seq")
     other = 1 - s
-    shards_in = (wq, wo, w1, w2)
+    near_x, near_y, corner = plane_peers(d)
+    shards_in = (wq.at[0], wq.at[1], wq.at[2], wo, w1, w2)
     full = (gq, go, g1, g2)
     pairs = ((x, gx), (c, gc), (sp, gsp))
 
     barrier = pltpu.get_barrier_semaphore()
-    for k in range(1, ndp):
-        pl.semaphore_signal(barrier, inc=1, device_id={"dp": lax.rem(d + k, ndp)}, device_id_type=MESH)
+    for peer in (near_x, near_y):
+        pl.semaphore_signal(barrier, inc=1, device_id={"dp": peer}, device_id_type=MESH)
     pl.semaphore_signal(barrier, inc=1, device_id={"seq": other}, device_id_type=MESH)
-    pl.semaphore_wait(barrier, ndp)
-
-    mine = shard_views(full, d * nseq + s, sizes)
-    far = []
-    near = []
-    for a in range(4):
-        for k in range(1, ndp):
-            copy = remote(
-                shards_in[a], mine[a], send.at[a, k], recv.at[a, k], {"dp": lax.rem(d + k, ndp)}
-            )
+    pl.semaphore_wait(barrier, 3)
+
+    mine = pieces(full, d * nseq + s, sizes)
+    from_x = pieces(full, near_x * nseq + s, sizes)
+    from_y = pieces(full, near_y * nseq + s, sizes)
+    from_corner = pieces(full, corner * nseq + s, sizes)
+    hops = {}
+    copies = []
+    locals_ = []
+    for a, x_first in slots(6):
+        order = ((0, near_x), (1, near_y)) if x_first else ((1, near_y), (0, near_x))
+        for way, peer in order:
+            copy = remote(shards_in[a], mine[a], send.at[a, way], recv.at[a, way], {"dp": peer})
             copy.start()
-            far.append((a, k, copy))
+            hops[a, way] = copy
     for j, (src, dst) in enumerate(pairs):
         copy = remote(src, dst.at[:, s], psend.at[j], precv.at[j], {"seq": other})
         copy.start()
-        near.append(copy)
-    here = []
-    for j, (src, dst) in enumerate(pairs):
+        copies.append(copy)
         copy = pltpu.make_async_copy(src, dst.at[:, s], plocal.at[j])
         copy.start()
-        here.append(copy)
-    for a in range(4):
+        locals_.append(copy)
+    for a, _ in slots(6):
         copy = remote(shards_in[a], mine[a], send2.at[a, 0], recv2.at[a, 0], {"seq": other})
         copy.start()
-        near.append(copy)
+        copies.append(copy)
         copy = pltpu.make_async_copy(shards_in[a], mine[a], local.at[a])
         copy.start()
-        here.append(copy)
-    for a, k, copy in far:
-        copy.wait_recv()
-        view = shard_views(full, lax.rem(d + ndp - k, ndp) * nseq + s, sizes)[a]
-        onward = remote(view, view, send2.at[a, k], recv2.at[a, k], {"seq": other})
-        onward.start()
-        near.append(onward)
-    for copy in here:
+        locals_.append(copy)
+
+    def across(a, slot, view):
+        copy = remote(view, view, send2.at[a, slot], recv2.at[a, slot], {"seq": other})
+        copy.start()
+        copies.append(copy)
+
+    last = {}
+    for a, x_first in slots(6):
+        for way in (0, 1) if x_first else (1, 0):
+            hops[a, way].wait_recv()
+            view = (from_x, from_y)[way][a]
+            if x_first == (way == 0):
+                peer = near_y if x_first else near_x
+                copy = remote(view, view, send.at[a, 2], recv.at[a, 2], {"dp": peer})
+                copy.start()
+                last[a] = copy
+            across(a, 1 + way, view)
+    for a, _ in slots(6):
+        last[a].wait_recv()
+        across(a, 3, from_corner[a])
+    for copy in locals_:
         copy.wait()
-    for _, _, copy in far:
+    for copy in hops.values():
         copy.wait_send()
-    for copy in near:
+    for copy in last.values():
+        copy.wait_send()
+    for copy in copies:
         copy.wait()
 
 
-def reduce_kernel(ndp, nt, sizes, *refs):
-    (pq, po, p1, p2, zin, bin_) = refs[:6]
-    (oq, oo, o1, o2, zout, bout) = refs[6:12]
-    own = refs[12:16]
-    got1 = refs[16:20]
-    got2 = refs[20:24]
-    zgot, bpair, bsum, bgot2, bsum2, bgot3 = refs[24:30]
-    (s1, r1, l1, s2, r2, zs, zr, as_, ar, b1s, b1r, b2s, b2r, b3s, b3r) = refs[30:]
+def across_tokens(left, right):
+    return lax.dot_general(
+        left, right, (((0,), (0,)), ((), ())), preferred_element_type=jnp.float32
+    )
+
+
+def reduce_kernel(nt, sizes, *refs):
+    (first, gproj, ctx, cot, second, ghid, hid, zbr, zgr, tokens, rowb, bin_) = refs[:12]
+    (oq, oo, o1, o2, yout, gout, bout) = refs[12:19]
+    give, own, got1, got2, got3 = (refs[19 + 6 * i : 25 + 6 * i] for i in range(5))
+    zgot, bpair, bsum, bgot2, bsum2, bgot3 = refs[49:55]
+    (s1, r1, s2, r2, zs, zr, as_, ar, b1s, b1r, b2s, b2r, b3s, b3r) = refs[55:]
     nseq = 2
-    partial = (pq, po, p1, p2)
-    outs = (oq, oo, o1, o2)
+    ndp = 4
     d, s, t = lax.axis_index("dp"), lax.axis_index("seq"), lax.axis_index("tensor")
     other = 1 - s
-    rows = zin.shape[1] // nt
+    near_x, near_y, corner = plane_peers(d)
+    rows = zbr.shape[0] // nt
+    outs = (oq.at[0], oq.at[1], oq.at[2], oo, o1, o2)
 
     barrier = pltpu.get_barrier_semaphore()
-    for k in range(1, ndp):
-        pl.semaphore_signal(barrier, inc=1, device_id={"dp": lax.rem(d + k, ndp)}, device_id_type=MESH)
+    for peer in (near_x, near_y, corner):
+        pl.semaphore_signal(barrier, inc=1, device_id={"dp": peer}, device_id_type=MESH)
     for k in range(1, nt):
         pl.semaphore_signal(
             barrier, inc=1, device_id={"tensor": lax.rem(t + k, nt)}, device_id_type=MESH
@@ -496,66 +529,126 @@
     def band(index):
         return pl.ds(pl.multiple_of(index * rows, rows), rows)
 
-    zsends = []
-    for k in range(1, nt):
-        peer = lax.rem(t + k, nt)
-        copy = remote(zin.at[:, band(peer)], zgot.at[k], zs.at[k], zr.at[k], {"tensor": peer})
-        copy.start()
-        zsends.append(copy)
-    first = {}
-    mine = {}
-    order = list(range(1, ndp)) + [0]
-    for k in order:
-        dest = lax.rem(d + k, ndp)
-        give = shard_views(partial, dest * nseq + other, sizes)
-        keep = shard_views(partial, dest * nseq + s, sizes)
-        for a in range(4):
-            copy = remote(give[a], got1[a].at[k], s1.at[a, k], r1.at[a, k], {"seq": other})
+    zsends = {}
+    for j, src in enumerate((zbr, zgr)):
+        for k in range(1, nt):
+            peer = lax.rem(t + k, nt)
+            copy = remote(
+                src.at[band(peer), :], zgot.at[j, k], zs.at[j, k], zr.at[j, k], {"tensor": peer}
+            )
             copy.start()
-            first[a, k] = copy
-            copy = pltpu.make_async_copy(keep[a], own[a].at[k], l1.at[a, k])
-            copy.start()
-            mine[a, k] = copy
+            zsends[j, k] = copy
     bpair_copy = remote(bin_, bpair, b1s, b1r, {"seq": other})
     bpair_copy.start()
 
-    second = {}
-    for k in order:
-        for a in range(4):
-            mine[a, k].wait()
-            first[a, k].wait_recv()
-            own[a][k] = (
-                own[a][k].astype(jnp.float32) + got1[a][k].astype(jnp.float32)
-            ).astype(own[a].dtype)
-            if k:
-                copy = remote(
-                    own[a].at[k], got2[a].at[k], s2.at[a, k], r2.at[a, k], {"dp": lax.rem(d + k, ndp)}
-                )
-                copy.start()
-                second[a, k] = copy
+    def product(a, index):
+        span = lambda n: pl.ds(pl.multiple_of(index * n, n), n)
+        if a < 3:
+            return across_tokens(first[:, span(sizes[0])], gproj[a])
+        if a == 3:
+            return across_tokens(ctx[...], cot[:, span(sizes[1])])
+        if a == 4:
+            return across_tokens(second[:, span(sizes[2])], ghid[...])
+        return across_tokens(hid[...], cot[:, span(sizes[3])])
+
+    places = (d, near_x, near_y, corner)
+    big_first = ((5, True), (4, False), (2, True), (0, False), (1, True), (3, False))
+    pair = {}
+    hop1 = {}
+    hop2 = {}
+
+    def make(where):
+        for a, _ in big_first:
+            give[a][where] = product(a, places[where] * nseq + other).astype(jnp.bfloat16)
+            copy = remote(
+                give[a].at[where], got1[a].at[where], s1.at[a, where], r1.at[a, where], {"seq": other}
+            )
+            copy.start()
+            pair[a, where] = copy
+        for a, _ in big_first:
+            own[a][where] = product(a, places[where] * nseq + s).astype(jnp.bfloat16)
+
+    def merge(a, where):
+        pair[a, where].wait_recv()
+        own[a][where] = (
+            own[a][where].astype(jnp.float32) + got1[a][where].astype(jnp.float32)
+        ).astype(jnp.bfloat16)
+
+    def hop(a, x_first, where, slot):
+        peer = near_x if x_first else near_y
+        copy = remote(
+            own[a].at[where], got2[a].at[slot], s2.at[a, slot], r2.at[a, slot], {"dp": peer}
+        )
+        copy.start()
+        hop1[a, slot] = copy
+
+    make(3)
+    make(1)
+    for a, x_first in big_first:
+        merge(a, 3)
+        hop(a, x_first, 3, 1)
+    make(2)
+    for a, x_first in big_first:
+        if x_first:
+            merge(a, 1)
+            hop(a, x_first, 1, 0)
+    for a, x_first in big_first:
+        if not x_first:
+            merge(a, 2)
+            hop(a, x_first, 2, 0)
+    make(0)
+    for a, x_first in big_first:
+        merge(a, 2 if x_first else 1)
+        merge(a, 0)
 
     bpair_copy.wait()
     bsum[...] = bin_[...] + bpair[...]
     bsends = []
-    for k in range(1, ndp):
-        copy = remote(bsum, bgot2.at[d], b2s.at[k], b2r.at[k], {"dp": lax.rem(d + k, ndp)})
+    for k, peer in ((1, near_x), (2, near_y), (3, corner)):
+        copy = remote(bsum, bgot2.at[d], b2s.at[k], b2r.at[k], {"dp": peer})
         copy.start()
         bsends.append(copy)
 
-    total = zin[:, band(t)].astype(jnp.float32)
-    for k, copy in zip(range(1, nt), zsends):
-        copy.wait_recv()
-        total = total + zgot[k].astype(jnp.float32)
-    zout[:, band(t)] = total.astype(zout.dtype)
+    for a, x_first in big_first:
+        hop1[a, 1].wait_recv()
+        mid = 2 if x_first else 1
+        own[a][mid] = (
+            own[a][mid].astype(jnp.float32) + got2[a][1].astype(jnp.float32)
+        ).astype(jnp.bfloat16)
+        copy = remote(
+            own[a].at[mid],
+            got3[a],
+            s2.at[a, 2],
+            r2.at[a, 2],
+            {"dp": near_y if x_first else near_x},
+        )
+        copy.start()
+        hop2[a] = copy
+    for a, _ in big_first:
+        hop1[a, 0].wait_recv()
+    zfull = []
+    for j, src in enumerate((zbr, zgr)):
+        total = src[band(t), :].astype(jnp.float32)
+        for k in range(1, nt):
+            zsends[j, k].wait_recv()
+            total = total + zgot[j, k].astype(jnp.float32)
+        zfull.append(total)
+    inputs = tokens[band(t), :].astype(jnp.float32)
+    _, normed, inv_std = layer_norm(inputs, 1.0, 0.0)
+    yout[band(t), :] = (inputs + zfull[0] + rowb[2:3, :] + rowb[3:4, :]).astype(yout.dtype)
+    gout[band(t), :] = norm_back(zfull[1], normed, inv_std, 1.0).astype(gout.dtype)
     asends = []
-    for k in range(1, nt):
-        peer = lax.rem(t + k, nt)
-        copy = remote(
-            zout.at[:, band(t)], zout.at[:, band(t)], as_.at[k], ar.at[k], {"tensor": peer}
-        )
-        copy.start()
-        asends.append(copy)
-
+    for j, dst in enumerate((yout, gout)):
+        for k in range(1, nt):
+            copy = remote(
+                dst.at[band(t), :],
+                dst.at[band(t), :],
+                as_.at[j, k],
+                ar.at[j, k],
+                {"tensor": lax.rem(t + k, nt)},
+            )
+            copy.start()
+            asends.append(copy)
     for copy in bsends:
         copy.wait()
     bgot2[d] = bsum[...]
@@ -569,13 +662,13 @@
         copy.start()
         bsends.append(copy)
 
-    for a in range(4):
-        acc = own[a][0].astype(jnp.float32)
-        for k in range(1, ndp):
-            second[a, k].wait_recv()
-            acc = acc + got2[a][k].astype(jnp.float32)
-        outs[a][...] = acc
-
+    for a, x_first in big_first:
+        hop2[a].wait_recv()
+        outs[a][...] = (
+            own[a][0].astype(jnp.float32)
+            + got2[a][0].astype(jnp.float32)
+            + got3[a][...].astype(jnp.float32)
+        )
     for copy in bsends:
         copy.wait()
     bgot3[t] = bsum2[...]
@@ -586,12 +679,9 @@
     bout[1] = whole
     for copy in asends:
         copy.wait()
-    for copy in zsends:
-        copy.wait_send()
-    for copy in first.values():
-        copy.wait_send()
-    for copy in second.values():
-        copy.wait_send()
+    for group in (zsends, pair, hop1, hop2):
+        for copy in group.values():
+            copy.wait_send()
 
 
 def gather_all(ndp, sizes, w_qkv, w_out, w_fc1, w_fc2, tokens, cotangent, ids):
@@ -600,7 +690,7 @@
     seqs, rows, width = tokens.shape
     dma = pltpu.SemaphoreType.DMA
     return pl.pallas_call(
-        functools.partial(gather_kernel, ndp, sizes),
+        functools.partial(gather_kernel, sizes),
         out_shape=(
             shape((w_qkv.shape[0], w_qkv.shape[1] * many, w_qkv.shape[2]), w_qkv.dtype),
             shape((w_out.shape[0], w_out.shape[1] * many), w_out.dtype),
@@ -613,11 +703,11 @@
         in_specs=[VM] * 7,
         out_specs=[ANY] * 7,
         scratch_shapes=[
-            dma((4, ndp)),
-            dma((4, ndp)),
-            dma((4, ndp)),
-            dma((4, ndp)),
-            dma((4,)),
+            dma((6, 3)),
+            dma((6, 3)),
+            dma((6, 4)),
+            dma((6, 4)),
+            dma((6,)),
             dma((3,)),
             dma((3,)),
             dma((3,)),
@@ -626,61 +716,67 @@
     )(w_qkv, w_out, w_fc1, w_fc2, tokens, cotangent, ids)
 
 
-def reduce_all(ndp, nt, sizes, partials, zin, bias_rows):
+def reduce_all(nt, sizes, operands, bias_rows):
     shape = jax.ShapeDtypeStruct
-    many = ndp * 2
-    pq, po, p1, p2 = partials
+    first, gproj, ctx, cot, second, ghid, hid, zbr = operands[:8]
     dma = pltpu.SemaphoreType.DMA
-    shards_shape = (
-        (pq.shape[0], pq.shape[1] // many, pq.shape[2]),
-        (po.shape[0], po.shape[1] // many),
-        (p1.shape[0] // many, p1.shape[1]),
-        (p2.shape[0], p2.shape[1] // many),
-    )
-    stacks = [pltpu.VMEM((ndp,) + part, jnp.bfloat16) for part in shards_shape]
-    rows = zin.shape[1] // nt
+    parts = ((sizes[0], gproj.shape[2]),) * 3 + (
+        (ctx.shape[1], sizes[1]),
+        (sizes[2], ghid.shape[1]),
+        (hid.shape[1], sizes[3]),
+    )
+    stack = lambda n: [pltpu.VMEM((n,) + part, jnp.bfloat16) for part in parts]
+    rows = zbr.shape[0] // nt
     bias_shape = bias_rows.shape
     return pl.pallas_call(
-        functools.partial(reduce_kernel, ndp, nt, sizes),
-        out_shape=tuple(shape(part, jnp.float32) for part in shards_shape)
-        + (shape(zin.shape, zin.dtype), shape((2,) + bias_shape, jnp.float32)),
-        in_specs=[ANY] * 4 + [VM] * 2,
-        out_specs=[VM] * 6,
-        scratch_shapes=stacks
-        + stacks
-        + stacks
+        functools.partial(reduce_kernel, nt, sizes),
+        out_shape=(
+            shape((3,) + parts[0], jnp.float32),
+            shape(parts[3], jnp.float32),
+            shape(parts[4], jnp.float32),
+            shape(parts[5], jnp.float32),
+            shape(zbr.shape, jnp.bfloat16),
+            shape(zbr.shape, jnp.bfloat16),
+            shape((2,) + bias_shape, jnp.float32),
+        ),
+        in_specs=[VM] * 12,
+        out_specs=[VM] * 7,
+        scratch_shapes=stack(4)
+        + stack(4)
+        + stack(4)
+        + stack(2)
+        + [pltpu.VMEM(part, jnp.bfloat16) for part in parts]
         + [
-            pltpu.VMEM((nt, zin.shape[0], rows, zin.shape[2]), zin.dtype),
+            pltpu.VMEM((2, nt, rows, zbr.shape[1]), jnp.bfloat16),
             pltpu.VMEM(bias_shape, jnp.float32),
             pltpu.VMEM(bias_shape, jnp.float32),
-            pltpu.VMEM((ndp,) + bias_shape, jnp.float32),
+            pltpu.VMEM((4,) + bias_shape, jnp.float32),
             pltpu.VMEM(bias_shape, jnp.float32),
             pltpu.VMEM((nt,) + bias_shape, jnp.float32),
-            dma((4, ndp)),
-            dma((4, ndp)),
-            dma((4, ndp)),
-            dma((4, ndp)),
-            dma((4, ndp)),
-            dma((nt,)),
-            dma((nt,)),
-            dma((nt,)),
-            dma((nt,)),
+            dma((6, 4)),
+            dma((6, 4)),
+            dma((6, 3)),
+            dma((6, 3)),
+            dma((2, nt)),
+            dma((2, nt)),
+            dma((2, nt)),
+            dma((2, nt)),
             dma,
             dma,
-            dma((ndp,)),
-            dma((ndp,)),
+            dma((4,)),
+            dma((4,)),
             dma((nt,)),
             dma((nt,)),
         ],
         compiler_params=pltpu.CompilerParams(collective_id=1, has_side_effects=True),
-    )(pq, po, p1, p2, zin, bias_rows)
+    )(*operands, bias_rows)
 
 
 def block(mesh, *args):
     seqs, rows, _ = args[0].shape
     heads = args[4].shape[2] // HD
     length = rows * mesh.shape["seq"]
-    if mesh.shape["seq"] == 2 and seqs * heads * length * length * 4 <= 2**23:
+    if mesh.shape["seq"] == 2 and mesh.shape["dp"] == 4 and seqs * heads * length * length * 4 <= 2**23:
         return whole_rows(mesh.shape["dp"], mesh.shape["tensor"], *args)
     return shards(*args)
 
@@ -781,12 +877,6 @@
     grad_hidden = grad_pre.astype(bf16)
     grad_second = jnp.einsum("ikq,uq->iku", grad_hidden, w1, preferred_element_type=f32)
     grad_first = jnp.einsum("etbp,eop->tbo", grad_proj_in, wq, preferred_element_type=f32)
-    partials = (
-        jnp.einsum("ink,oint->okt", first, grad_proj_in, preferred_element_type=f32).astype(bf16),
-        jnp.einsum("bxz,bxe->ze", context_here, cotangent, preferred_element_type=f32).astype(bf16),
-        jnp.einsum("mxa,mxr->ar", second, grad_hidden, preferred_element_type=f32).astype(bf16),
-        jnp.einsum("tzi,tzo->io", hidden, cotangent, preferred_element_type=f32).astype(bf16),
-    )
     scaled = grad_first * ln_gains[0] + grad_second * ln_gains[1]
     hid = w_fc1.shape[1]
     wide = max(width, hid, qkv_bias.size)
@@ -803,13 +893,23 @@
             jnp.zeros((wide,), f32),
         ]
     )
-    zin = jnp.stack([branches, scaled]).astype(bf16).reshape(2, seqs * rows, width)
-    gq, go, g1, g2, zsum, bias = reduce_all(ndp, nt, sizes, partials, zin, bias_rows)
-    zsum = zsum.astype(f32).reshape(2, seqs, rows, width)
-    output = (inputs_f + zsum[0] + row_biases[2] + row_biases[3]).astype(bf16)
-    centre = jnp.mean(zsum[1], axis=-1, keepdims=True)
-    slope = jnp.mean(zsum[1] * normed, axis=-1, keepdims=True)
-    grad_input = grad_f + inv_std * (zsum[1] - centre - normed * slope)
+    tall = lambda v: v.reshape(seqs * rows, -1).astype(bf16)
+    operands = (
+        tall(first),
+        grad_proj_in.reshape(3, seqs * rows, flat),
+        tall(context_here),
+        tall(cotangent),
+        tall(second),
+        tall(grad_hidden),
+        tall(hidden),
+        tall(branches),
+        tall(scaled),
+        tall(block_input),
+        row_biases,
+    )
+    gq, go, g1, g2, output, grad_norm, bias = reduce_all(nt, sizes, operands, bias_rows)
+    output = output.reshape(seqs, rows, width)
+    grad_input = grad_f + grad_norm.reshape(seqs, rows, width).astype(f32)
     total = bias[1, :, :width]
     grad_ct = bias[0, 6, :width]
     return (

time: 148 us -> 146 us (0.986)
  Pallas kernels: 99.6 us -> 92.8 us
  other arithmetic: 10.3 us -> 13.9 us
  local copies, waits for them, and re-layouts: 14.3 us -> 16.7 us
  matrix products: 21.9 us -> 19.9 us
    dot_general x4 -> x0, matrix products: 7.53 us -> none  [the longest x1 2.24 us: whole_rows(): jnp.einsum('mxa,mxr->ar', second, grad_hidden, preferred_element_type=f32)]
    pallas_call x2, Pallas kernels: 99.6 us -> 92.8 us  [the longest x1 58.1 us: reduce_all(): pl.pallas_call(functools.partial(reduce_kernel, nt, sizes), out_shape=(sh...]
    sub x1, matrix products: 1.11 us -> 2.98 us  [whole_rows(): expo = jnp.where(allowed, jnp.exp(scores - row_max), 0.0)]
    dot_general x1, matrix products: 2.37 us -> 0.7 us  [whole_rows(): jnp.einsum('qzg,gc->qzc', hidden, w2, preferred_element_type=f32)]
    unnamed x58 -> x90, local copies, waits for them, and re-layouts: 6.12 us -> 7.77 us
where the time goes in v2:
time: 146 us; the launch traced here: 145 us
  Pallas kernels  92.8 us (64%)
  matrix products  19.9 us (14%)
  local copies, waits for them, and re-layouts  16.7 us (11%)
  other arithmetic  13.9 us (10%)
    pallas_call x1, Pallas kernels, reduce_all(): pl.pallas_call(functools.partial(reduce_kernel, nt, sizes), out_shape=(sh...  58.1 us
    pallas_call x1, Pallas kernels, gather_all(): pl.pallas_call(functools.partial(gather_kernel, sizes), out_shape=(shape(...  34.7 us
    unnamed x90, local copies, waits for them, and re-layouts  7.77 us
    sub x1, matrix products, whole_rows(): expo = jnp.where(allowed, jnp.exp(scores - row_max), 0.0)  2.98 us

profile of v2, /device:TPU:0, one launch (start us, length us, event | category | flops | bytes accessed | tf_op | source)
XLA Modules:
  0.0 144.6 jit_solution(12524907952445364949)
XLA Ops:
  0.7 1.2 convert_reduce_fusion.1
  1.9 1.3 fusion.52
  3.2 1.3 pad_add_fusion.refs_6_
  4.5 1.1 convert_reduce_fusion
  5.6 0.8 fusion.92
  6.4 0.8 fusion.91
  7.3 1.3 fusion.49
  8.6 34.7 %shard_map.195 = (bf16[3,1024,256]{2,1,0:T(8,128)(2,1)}, bf16[256,1024]{1,0:T(8,128)(2,1)}, bf16[1024,1024]{1,0:T(8,128)(2,1)}, bf16[1024,1024]{1,0:T(8,128)(2,1...) custom-call(bf16[3,128,256]{2,1,0:T(8,128)(2,1)} %refs_0_.1, ...), custom_call_target="tpu_custom_call" | custom-call | tf_op jit(solution)/shard_map/pallas_call | solution.py:692
  43.3 2.6 %convolution_convert_fusion = bf16[2,256,256]{1,2,0:T(8,128)(2,1)} fusion(bf16[2,256,1024]{2,1,0:T(8,128)(2,1)} %bitcast.210, bf16[256,1024]{1,0:T(8,128)(2,1)} %get-tuple-element.28), kind=kOutput, calls=%fused_computation.49 | convolution fusion | flops 268566528 | bytes 1835008 | tf_op jit(solution)/shard_map/sli,zi->slz/dot_general | solution.py:845
  48.7 0.8 compare_and_fusion
  49.5 1.0 add_bitcast_fusion
  52.3 0.8 multiply_convert_fusion.1
  53.3 0.7 copy-done.6
  54.0 2.4 %fusion.88 = (f32[1024]{0:T(1024)}, bf16[2,128,1024]{2,1,0:T(8,128)(2,1)}) fusion(f32[2,128,1024]{2,1,0:T(8,128)S(1)} %get-tuple-element.82, bf16[2,128,1024]{2,1,0:T(8,128)(2,1)S(1)} %copy-done.2, bf16[1024,1024]{1,0:T(8,128)(2,1)S(1)} %copy-done.6), kind=kOutput, calls=%fused_computation.143 | convolution fusion | flops 539753472 | bytes 4198400 | tf_op jit(solution)/shard_map/hvg,rg->hvr/dot_general | solution.py:876
  57.1 3.0 %fusion.93 = (f32[2,4,256]{2,1,0:T(4,128)}, f32[2,4,256,256]{2,3,1,0:T(8,128)S(1)}) fusion(pred[2,256,256]{1,2,0:T(8,128)(4,1)} %compare_and_fusion, bf16[2,256,4,48]{1,3,2,0:T(8,128)(2,1)} %slice.199, bf16[2,256,4,16]{1,3,2,0:T(8,128)(2,1)S(1)} %get-tuple-element.63, bf16[2,256,4,48]{1,3,2,0:T(8,128)(2,1)} %slice.200, ...), kind=kOutput, calls=%fused_computation.148 | convolution fusion | flops 139460864 | bytes 2760704 | tf_op jit(solution)/shard_map/sub | solution.py:841
  60.1 1.9 %multiply_reduce_fusion.1 = (f32[2,256,4]{1,2,0:T(4,128)}, bf16[2,256,4,64]{1,3,2,0:T(8,128)(2,1)S(1)}) fusion(bf16[2,256,256]{1,2,0:T(8,128)(2,1)} %convolution_convert_fusion, f32[2,256,4]{1,2,0:T(4,128)} %bitcast.197, bf16[2,256,4,64]{1,3,2,0:T(8,128)(2,1)S(1)} %bitcast.172, f32[2,4,256,256]{2,3,1,0:T(8,128)S(1)} %get-tuple-element.78), kind=kOutput, calls=%fused_computation.80 | convolution fusion | flops 68417536 | bytes 2899968 | tf_op jit(solution)/shard_map/shqk,skhd->shqd/dot_general | solution.py:843
  62.1 1.1 fusion.35
  63.2 0.8 copy.44
  64.0 1.5 %fusion.57 = f32[2,4,64,256]{3,2,1,0:T(8,128)S(1)} fusion(bf16[2,256,4,64]{1,3,2,0:T(8,128)(2,1)} %bitcast.184, f32[2,4,256,256]{2,3,1,0:T(8,128)S(1)} %get-tuple-element.78, f32[2,4,256]{2,1,0:T(4,128)} %get-tuple-element.77), kind=kOutput, calls=%fused_computation.65 | convolution fusion | flops 68157440 | bytes 2891776 | tf_op jit(solution)/shard_map/shqk,sqhd->skhd/dot_general | solution.py:853
  66.3 1.4 fusion.42
  70.9 0.7 copy-done.36
  71.7 2.1 %fusion.85 = (f32[1024]{0:T(1024)S(1)}, f32[1024]{0:T(1024)S(1)}, bf16[2,128,1024]{2,1,0:T(8,128)(2,1)}, f32[1024]{0:T(1024)S(1)}, f32[1024]{0:T(1024)S(1)}, /*index=5*/bf16[2,128,1024]{2,1,0:T(8,128)(2,1)}) fusion(f32[2,128]{1,0:T(2,128)S(1)} %copy-done.34, f32[2,128]{1,0:T(2,128)S(1)} %copy-done.29, bf16[2,128,1024]{2,1,0:T(8,128)(2,1)S(1)} %copy-done, ...), kind=kOutput, calls=%fused_computation.140 | convolution fusion | flops 541061120 | bytes 5273600 | tf_op jit(solution)/shard_map/ikq,uq->iku/dot_general | solution.py:878
  74.5 1.0 pad_maximum_fusion.3.refs_1_
  75.5 58.1 %shard_map.196 = (f32[3,128,256]{2,1,0:T(8,128)}, f32[256,128]{1,0:T(8,128)}, f32[128,1024]{1,0:T(8,128)}, f32[1024,128]{1,0:T(8,128)}, bf16[256,1024]{1,0:T(8,1...) custom-call(bf16[256,1024]{1,0:T(8,128)(2,1)} %bitcast.177, bf16[3,256,256]{2,1,0:T(8,128)(2,1)} %pad_maximum_fusion.3.refs_1_, ...), custom_call_target="tpu_custom_call" | custom-call | tf_op jit(solution)/shard_map/pallas_call | solution.py:731
  133.6 0.8 slice_reduce_fusion
  135.1 1.4 slice_bitcast_fusion
  136.4 1.4 slice_bitcast_fusion.3
  138.5 2.2 %convert_add_fusion = f32[2,128,1024]{2,1,0:T(8,128)} fusion(bf16[2,128,1024]{2,1,0:T(8,128)(2,1)S(1)} %copy-done.3, bf16[2,128,1024]{2,1,0:T(8,128)(2,1)} %bitcast.183), kind=kLoop, calls=%fused_computation.31 | loop fusion | flops 786432 | bytes 2097152 | tf_op jit(solution)/shard_map/add | solution.py:912
  140.8 0.8 copy.60
  141.6 0.7 copy.61
  143.0 0.8 copy.63
  143.8 0.8 copy.64
  (130 shorter events, 11.8 us)
Async XLA Ops:
  1.9 44.1 %copy-start.28 = (f32[2,128]{1,0:T(2,128)}, f32[2,128]{1,0:T(2,128)S(1)}, u32[]{:S(2)}) copy-start(f32[2,128]{1,0:T(2,128)S(1)} %broadcast_multiply_fusion.1) | copy-start | bytes 3076
  3.2 42.7 %copy-start.33 = (f32[2,128]{1,0:T(2,128)}, f32[2,128]{1,0:T(2,128)S(1)}, u32[]{:S(2)}) copy-start(f32[2,128]{1,0:T(2,128)S(1)} %add_rsqrt_fusion) | copy-start | bytes 3076
  8.6 43.6 %copy-start.7 = (bf16[2,128,1024]{2,1,0:T(8,128)(2,1)}, bf16[2,128,1024]{2,1,0:T(8,128)(2,1)S(1)}, u32[]{:S(2)}) copy-start(bf16[2,128,1024]{2,1,0:T(8,128)(2,1)S(1)} %fusion.49) | copy-start | bytes 1572868
  43.3 4.0 %copy-start.1 = (bf16[2,2,128,1024]{3,2,1,0:T(8,128)(2,1)S(1)}, bf16[2,2,128,1024]{3,2,1,0:T(8,128)(2,1)}, u32[]{:S(2)}) copy-start(bf16[2,2,128,1024]{3,2,1,0:T(8,128)(2,1)} %get-tuple-element.25) | copy-start | bytes 3145732
  47.3 2.1 %copy-start.8 = (bf16[3,1024,256]{2,1,0:T(8,128)(2,1)S(1)}, bf16[3,1024,256]{2,1,0:T(8,128)(2,1)}, u32[]{:S(2)}) copy-start(bf16[3,1024,256]{2,1,0:T(8,128)(2,1)} %get-tuple-element.24) | copy-start | bytes 4718596
  47.4 2.1 %copy-start.37 = (f32[3,256]{1,0:T(4,128)S(1)}, f32[3,256]{1,0:T(4,128)}, u32[]{:S(2)}) copy-start(f32[3,256]{1,0:T(4,128)} %param.17) | copy-start | bytes 9220
  48.6 2.1 %copy-start.18 = (f32[2,256,16]{1,2,0:T(8,128)}, f32[2,256,16]{1,2,0:T(8,128)S(1)}, u32[]{:S(2)}) copy-start(f32[2,256,16]{1,2,0:T(8,128)S(1)} %get-tuple-element.85) | copy-start | bytes 98308
  48.6 2.1 %copy-start.20 = (f32[2,256,16]{1,2,0:T(8,128)}, f32[2,256,16]{1,2,0:T(8,128)S(1)}, u32[]{:S(2)}) copy-start(f32[2,256,16]{1,2,0:T(8,128)S(1)} %get-tuple-element.86) | copy-start | bytes 98308
  50.6 1.7 %copy-start.35 = (bf16[1024,1024]{1,0:T(8,128)(2,1)S(1)}, bf16[1024,1024]{1,0:T(8,128)(2,1)}, u32[]{:S(2)}) copy-start(bf16[1024,1024]{1,0:T(8,128)(2,1)} %get-tuple-element.30) | copy-start | bytes 6291460
  50.6 1.7 %copy-start.38 = (f32[1024]{0:T(1024)S(1)}, f32[1024]{0:T(1024)}, u32[]{:S(2)}) copy-start(f32[1024]{0:T(1024)} %param.20) | copy-start | bytes 12292
  50.8 6.4 %copy-start.22 = (bf16[2,256,4,16]{1,3,2,0:T(8,128)(2,1)}, bf16[2,256,4,16]{1,3,2,0:T(8,128)(2,1)S(1)}, u32[]{:S(2)}) copy-start(bf16[2,256,4,16]{1,3,2,0:T(8,128)(2,1)S(1)} %get-tuple-element.62) | copy-start | bytes 196612
  50.8 6.4 %copy-start.24 = (bf16[2,256,4,16]{1,3,2,0:T(8,128)(2,1)}, bf16[2,256,4,16]{1,3,2,0:T(8,128)(2,1)S(1)}, u32[]{:S(2)}) copy-start(bf16[2,256,4,16]{1,3,2,0:T(8,128)(2,1)S(1)} %get-tuple-element.63) | copy-start | bytes 196612
  52.3 1.8 %copy-start.6 = (bf16[1024,1024]{1,0:T(8,128)(2,1)S(1)}, bf16[1024,1024]{1,0:T(8,128)(2,1)}, u32[]{:S(2)}) copy-start(bf16[1024,1024]{1,0:T(8,128)(2,1)} %get-tuple-element.29) | copy-start | bytes 6291460
  53.1 3.3 %copy-start.5 = (bf16[2,128,1024]{2,1,0:T(8,128)(2,1)}, bf16[2,128,1024]{2,1,0:T(8,128)(2,1)S(1)}, u32[]{:S(2)}) copy-start(bf16[2,128,1024]{2,1,0:T(8,128)(2,1)S(1)} %get-tuple-element.81) | copy-start | bytes 1572868
  60.1 1.9 %copy-start.12 = (bf16[256,1024]{1,0:T(8,128)(2,1)S(1)}, bf16[256,1024]{1,0:T(8,128)(2,1)}, u32[]{:S(2)}) copy-start(bf16[256,1024]{1,0:T(8,128)(2,1)} %get-tuple-element.28) | copy-start | bytes 1572868
  64.0 1.5 %copy-start.26 = (bf16[2,256,256]{1,2,0:T(8,128)(2,1)S(1)}, bf16[2,256,256]{1,2,0:T(8,128)(2,1)}, u32[]{:S(2)}) copy-start(bf16[2,256,256]{1,2,0:T(8,128)(2,1)} %convolution_convert_fusion) | copy-start | bytes 786436
  64.0 1.5 %copy-start.30 = (f32[2,4,256]{2,1,0:T(4,128)S(1)}, f32[2,4,256]{2,1,0:T(4,128)}, u32[]{:S(2)}) copy-start(f32[2,4,256]{2,1,0:T(4,128)} %get-tuple-element.77) | copy-start | bytes 24580
  64.0 1.5 %copy-start.31 = (f32[2,256,4]{1,2,0:T(4,128)S(1)}, f32[2,256,4]{1,2,0:T(4,128)}, u32[]{:S(2)}) copy-start(f32[2,256,4]{1,2,0:T(4,128)} %get-tuple-element.79) | copy-start | bytes 24580
  66.0 1.7 %copy-start.10 = (bf16[2,256,4,48]{1,3,2,0:T(8,128)(2,1)S(1)}, bf16[2,256,4,48]{1,3,2,0:T(8,128)(2,1)}, u32[]{:S(2)}) copy-start(bf16[2,256,4,48]{1,3,2,0:T(8,128)(2,1)} %slice.200) | copy-start | bytes 589828
  66.0 1.7 %copy-start.23 = (bf16[2,256,4,16]{1,3,2,0:T(8,128)(2,1)S(1)}, bf16[2,256,4,16]{1,3,2,0:T(8,128)(2,1)}, u32[]{:S(2)}) copy-start(bf16[2,256,4,16]{1,3,2,0:T(8,128)(2,1)} %copy-done.22) | copy-start | bytes 196612
  66.2 1.8 %copy-start.21 = (f32[2,256,16]{1,2,0:T(8,128)S(1)}, f32[2,256,16]{1,2,0:T(8,128)}, u32[]{:S(2)}) copy-start(f32[2,256,16]{1,2,0:T(8,128)} %copy-done.20) | copy-start | bytes 98308
  66.3 1.8 %copy-start.19 = (f32[2,256,16]{1,2,0:T(8,128)S(1)}, f32[2,256,16]{1,2,0:T(8,128)}, u32[]{:S(2)}) copy-start(f32[2,256,16]{1,2,0:T(8,128)} %copy-done.18) | copy-start | bytes 98308
  68.5 1.6 %copy-start.9 = (bf16[3,1024,256]{2,1,0:T(8,128)(2,1)S(1)}, bf16[3,1024,256]{2,1,0:T(8,128)(2,1)}, u32[]{:S(2)}) copy-start(bf16[3,1024,256]{2,1,0:T(8,128)(2,1)} %get-tuple-element.24) | copy-start | bytes 4718596
  69.8 1.9 %copy-start.36 = (bf16[1024,1024]{1,0:T(8,128)(2,1)S(1)}, bf16[1024,1024]{1,0:T(8,128)(2,1)}, u32[]{:S(2)}) copy-start(bf16[1024,1024]{1,0:T(8,128)(2,1)} %get-tuple-element.30) | copy-start | bytes 6291460
  71.7 2.2 %copy-start.32 = (f32[1024]{0:T(1024)S(1)}, f32[1024]{0:T(1024)}, u32[]{:S(2)}) copy-start(f32[1024]{0:T(1024)} %get-tuple-element.47) | copy-start | bytes 12292
  71.7 2.9 %copy-start.16 = (bf16[2,128,256]{2,1,0:T(8,128)(2,1)S(1)}, bf16[2,128,256]{2,1,0:T(8,128)(2,1)}, u32[]{:S(2)}) copy-start(bf16[2,128,256]{2,1,0:T(8,128)(2,1)} %convert.36) | copy-start | bytes 393220
  75.5 63.0 %copy-start.3 = (bf16[2,128,1024]{2,1,0:T(8,128)(2,1)S(1)}, bf16[2,128,1024]{2,1,0:T(8,128)(2,1)}, u32[]{:S(2)}) copy-start(bf16[2,128,1024]{2,1,0:T(8,128)(2,1)} %refs_5_.1) | copy-start | bytes 1572868
  133.6 7.1 %copy-start.15 = (bf16[256,1024]{1,0:T(8,128)(2,1)S(1)}, bf16[256,1024]{1,0:T(8,128)(2,1)}, u32[]{:S(2)}) copy-start(bf16[256,1024]{1,0:T(8,128)(2,1)} %get-tuple-element.31) | copy-start | bytes 1572868
  133.6 7.9 %copy-start.17 = (f32[3,128,256]{2,1,0:T(8,128)S(1)}, f32[3,128,256]{2,1,0:T(8,128)}, u32[]{:S(2)}) copy-start(f32[3,128,256]{2,1,0:T(8,128)} %get-tuple-element.99) | copy-start | bytes 1179652
  133.6 8.7 %copy-start.27 = (f32[256,128]{1,0:T(8,128)S(1)}, f32[256,128]{1,0:T(8,128)}, u32[]{:S(2)}) copy-start(f32[256,128]{1,0:T(8,128)} %get-tuple-element.100) | copy-start | bytes 393220
  138.5 4.5 %copy-start.14 = (f32[128,1024]{1,0:T(8,128)S(1)}, f32[128,1024]{1,0:T(8,128)}, u32[]{:S(2)}) copy-start(f32[128,1024]{1,0:T(8,128)} %get-tuple-element.101) | copy-start | bytes 1572868
  140.8 3.0 %copy-start.13 = (f32[1024,128]{1,0:T(8,128)S(1)}, f32[1024,128]{1,0:T(8,128)}, u32[]{:S(2)}) copy-start(f32[1024,128]{1,0:T(8,128)} %get-tuple-element.102) | copy-start | bytes 1572868
  (8 other events, 8.3 us)
